TPU v7x, 32 devices: a whole 2x2x4 slice. The times are simulated.
32 devices in a mesh: space: 8 (over z, y), samp: 4 (over x, core).
Axes of the slice: x: 2, y: 2, z: 4, core: 2. Of those that a mesh axis runs over, the one named last changes fastest.
Arguments:
- volume: bfloat16 [4, 32, 32, 256], P(None, 'space', 'samp'), may hold values from -6 to 6
- filters_one: bfloat16 [1728], P('samp'), may hold values from -0.625 to 0.625
- filters_two: bfloat16 [13824], P('space'), may hold values from -0.3125 to 0.3125
- cotangent: bfloat16 [32, 32, 32, 256], P(None, 'space', 'samp'), may hold values from -6 to 6
Outputs:
- activation: bfloat16 [32, 32, 32, 256], P(None, 'space', 'samp')
- grad_one: float32 [1728], P('samp')
- grad_two: float32 [13824], P('space')
All inputs are finite; a program needn't handle non-finite values.
Results may differ from a plain program's by a relative error of at most 0.0044.
The roundings to bfloat16 on the way count: a program that leaves them out, or rounds other values in their place, can miss the bound.
Values may be sent and summed in bfloat16 or wider, within the bound.
A program may use at most 64 MiB of HBM per device.

v0:
```python
import math

import jax
import jax.numpy as jnp
from jax import lax
from jax.sharding import PartitionSpec as P

CIN = 4
C1 = 16
C2 = 32


SLOPE = 0.3


def with_halo(cells, sides, width):
    for axis, dim in sides:
        count = lax.axis_size(axis)
        ends = count - 1
        head = lax.slice_in_dim(cells, 0, width, axis=dim)
        tail = lax.slice_in_dim(cells, cells.shape[dim] - width, cells.shape[dim], axis=dim)
        cells = jnp.concatenate(
            [
                lax.ppermute(tail, axis, [(i, (i + 1) % count) for i in range(ends)]),
                cells,
                lax.ppermute(head, axis, [((i + 1) % count, i) for i in range(ends)]),
            ],
            axis=dim,
        )
    return cells


def conv_valid(padded, kernel):
    result = lax.conv_general_dilated(
        padded[None],
        kernel,
        (1, 1, 1),
        "VALID",
        dimension_numbers=("NCDHW", "OIDHW", "NCDHW"),
        preferred_element_type=jnp.float32,
    )
    return result[0]


def kernel_grad(grad_out, padded):
    chans_out = grad_out.shape[0]
    chans_in = padded.shape[0]
    size_x, size_y, size_z = (grad_out.shape[1], grad_out.shape[2], grad_out.shape[3])
    flat_out = grad_out.reshape(chans_out, -1)
    pieces = []
    for shift_x in range(3):
        for shift_y in range(3):
            for shift_z in range(3):
                window = padded[
                    :,
                    shift_x : shift_x + size_x,
                    shift_y : shift_y + size_y,
                    shift_z : shift_z + size_z,
                ].reshape(chans_in, -1)
                pieces.append(
                    lax.dot_general(
                        flat_out,
                        window,
                        (((1,), (1,)), ((), ())),
                        preferred_element_type=jnp.float32,
                    )
                )
    return jnp.stack(pieces, axis=-1).reshape(-1)


def leaky(values):
    return jnp.where(values > 0, values, SLOPE * values)


def slope_of(values):
    return jnp.where(values > 0, jnp.float32(1.0), jnp.float32(SLOPE))


def pad_depth(field):
    return jnp.pad(field, ((0, 0), (0, 0), (0, 0), (1, 1)))


def on_device(volume, filters_one, filters_two, cotangent):
    size_x, size_y, size_z = (volume.shape[1], volume.shape[2], volume.shape[3])
    n_space = lax.axis_size("space")
    n_samp = lax.axis_size("samp")
    kernel_one = lax.all_gather(filters_one, "samp", axis=0, tiled=True).reshape(C1, CIN, 3, 3, 3)
    kernel_two = lax.all_gather(filters_two, "space", axis=0, tiled=True).reshape(C2, C1, 3, 3, 3)
    flipped = jnp.flip(kernel_two, (2, 3, 4)).transpose(1, 0, 2, 3, 4)
    volume_pad = pad_depth(with_halo(volume, (("space", 1), ("samp", 2)), 1))
    pre_one = conv_valid(volume_pad, kernel_one)
    hidden = leaky(pre_one).astype(jnp.bfloat16)
    hidden_pad = pad_depth(with_halo(hidden, (("space", 1), ("samp", 2)), 1))
    pre_two = conv_valid(hidden_pad, kernel_two)
    back_two = (cotangent.astype(jnp.float32) * slope_of(pre_two)).astype(jnp.bfloat16)
    back_pad = pad_depth(with_halo(back_two, (("space", 1), ("samp", 2)), 1))
    activation = leaky(pre_two).astype(jnp.bfloat16)
    dhidden = conv_valid(back_pad, flipped)
    back_one = (dhidden * slope_of(pre_one)).astype(jnp.bfloat16)
    term_two = kernel_grad(back_two, hidden_pad)
    term_one = kernel_grad(back_one, volume_pad)
    scale = 1.0 / math.sqrt(float(size_x * n_space * size_y * n_samp * size_z))
    length_two = term_two.shape[0] // n_space
    length_one = term_one.shape[0] // n_samp
    total_one, total_two = lax.psum((term_one, term_two), ("space", "samp"))
    grad_two = (
        lax.dynamic_slice_in_dim(total_two, lax.axis_index("space") * length_two, length_two)
        * scale
    )
    grad_one = (
        lax.dynamic_slice_in_dim(total_one, lax.axis_index("samp") * length_one, length_one) * scale
    )
    return (activation, grad_one, grad_two)


def solution(mesh):
    in_specs = (
        P(None, "space", "samp", None),
        P("samp"),
        P("space"),
        P(None, "space", "samp", None),
    )
    out_specs = (P(None, "space", "samp", None), P("samp"), P("space"))
    return jax.shard_map(
        on_device, mesh=mesh, in_specs=in_specs, out_specs=out_specs, check_vma=False
    )
```

profile of v0, /device:TPU:0, one launch (start us, length us, event | category | flops | bytes accessed | tf_op | source)
XLA Modules:
  0.0 227.9 jit_solution(9096770704066738644)
XLA Ops:
  0.6 0.9 copy.86
  1.5 4.9 %collective-permute-start = (bf16[4,1,8,256]{3,0,2,1:T(4,128)(2,1)S(1)}, bf16[4,1,8,256]{3,0,2,1:T(4,128)(2,1)S(1)}, u32[]{:S(2)}, u32[]{:S(2)}) collective-permute-start(bf16[4,1,8,256]{3,0,2,1:T(4,128)(2,1)S(1)} %get-tuple-element.29), channel_id=1, source_target_pairs={{0,4},{4,8},{8,12},{12,16},{16,20},{20,24},{24,28},{1,5},{5,9},{9,... | collective-permute-start | bytes 49160 | tf_op jit(solution)/shard_map/ppermute | solution.py:24
  6.4 1.3 collective-permute-start.1
  7.9 0.9 constant_dynamic-update-slice_fusion.1
  8.8 3.3 %collective-permute-done.1 = bf16[4,1,8,256]{3,0,2,1:T(4,128)(2,1)S(1)} collective-permute-done((bf16[4,1,8,256]{3,0,2,1:T(4,128)(2,1)S(1)}, bf16[4,1,8,256]{3,0,2,1:T(4,128)(2,1)S(1)}, u32[]{:S(2)}, u32[]{:S(2)}) %collective-permute-start.1) | collective-permute-done | bytes 16416 | tf_op jit(solution)/shard_map/ppermute | solution.py:26
  12.1 1.3 collective-permute-start.3
  13.4 3.0 %collective-permute-start.2 = (bf16[4,6,1,256]{3,0,2,1:T(4,128)(2,1)S(1)}, bf16[4,6,1,256]{3,0,2,1:T(4,128)(2,1)S(1)}, u32[]{:S(2)}, u32[]{:S(2)}) collective-permute-start(bf16[4,6,1,256]{3,0,2,1:T(4,128)(2,1)S(1)} %get-tuple-element.26), channel_id=1, source_target_pairs={{0,1},{1,2},{2,3},{4,5},{5,6},{6,7},{8,9},{9,10},{10,11},{12,13},{... | collective-permute-start | bytes 36872 | tf_op jit(solution)/shard_map/ppermute | solution.py:24
  16.5 1.2 dynamic-slice
  18.4 0.9 dynamic-update-slice
  19.2 6.8 %all-reduce.3 = bf16[1728]{0:T(1024)(128)(2,1)S(1)} all-reduce(bf16[1728]{0:T(1024)(128)(2,1)S(1)} %dynamic-update-slice), channel_id=1, replica_groups=mesh['space'=8,'samp'=4] {'samp'}, use_global_device_ids=true, to_apply=%add.3 | all-reduce | flops 1728 | bytes 6912
  26.4 0.3 copy.91
  27.0 0.4 reshape.17
  27.4 1.8 copy.90
  29.4 10.7 %broadcast_select_fusion.2 = f32[4,8,8,33,16]{4,2,3,1,0:T(8,128)} fusion(pred[8,33]{0,1:T(8,128)(4,1)S(1)} %copy-done.13, bf16[16,4,3,3,3]{0,1,4,3,2:T(4,128)(2,1)S(1)} %copy.91, bf16[4,6,10,1,7,2]{4,0,5,2,1,3:T(4,128)(2,1)S(1)} %slice.308, bf16[4,6,10,1,8,33]{4,0,5,2,1,3:T(4,128)(2,1)S(1)} %copy.90), kind=kOutput, calls=%fused_computation.25 | convolution fusion | flops 29734656 | bytes 677832 | tf_op jit(solution)/shard_map/conv_general_dilated | solution.py:34
  40.1 4.2 %copy.92 = f32[4,8,8,33,16]{3,2,4,1,0:T(8,128)S(1)} copy(f32[4,8,8,33,16]{4,2,3,1,0:T(8,128)} %broadcast_select_fusion.2) | data formatting | bytes 1081344 | tf_op jit(solution)/shard_map/conv_general_dilated | solution.py:34
  44.3 0.6 reshape.21
  45.0 1.3 collective-permute-start.5
  46.3 5.0 %collective-permute-start.4 = (bf16[16,1,8,256]{3,0,2,1:T(8,128)(2,1)S(1)}, bf16[16,1,8,256]{3,0,2,1:T(8,128)(2,1)S(1)}, u32[]{:S(2)}, u32[]{:S(2)}) collective-permute-start(bf16[16,1,8,256]{3,0,2,1:T(8,128)(2,1)S(1)} %get-tuple-element.24), channel_id=1, source_target_pairs={{0,4},{4,8},{8,12},{12,16},{16,20},{20,24},{24,28},{1,5},{5,9},{9,... | collective-permute-start | bytes 196616 | tf_op jit(solution)/shard_map/ppermute | solution.py:24
  51.3 0.6 dynamic-slice.1
  52.6 0.3 dynamic-update-slice.1
  52.9 36.0 %all-reduce.4 = bf16[13824]{0:T(1024)(128)(2,1)S(1)} all-reduce(bf16[13824]{0:T(1024)(128)(2,1)S(1)} %dynamic-update-slice.1), channel_id=1, replica_groups=mesh['space'=8,'samp'=4] {'space'}, use_global_device_ids=true, to_apply=%add.4 | all-reduce | flops 13824 | bytes 55296
  88.9 1.6 reshape.9
  90.5 2.2 copy.95
  92.8 1.3 collective-permute-start.7
  94.1 3.2 %collective-permute-start.6 = (bf16[16,6,1,256]{3,0,2,1:T(8,128)(2,1)S(1)}, bf16[16,6,1,256]{3,0,2,1:T(8,128)(2,1)S(1)}, u32[]{:S(2)}, u32[]{:S(2)}) collective-permute-start(bf16[16,6,1,256]{3,0,2,1:T(8,128)(2,1)S(1)} %get-tuple-element.22), channel_id=1, source_target_pairs={{0,1},{1,2},{2,3},{4,5},{5,6},{6,7},{8,9},{9,10},{10,11},{12,13},{... | collective-permute-start | bytes 147464 | tf_op jit(solution)/shard_map/ppermute | solution.py:24
  97.3 0.8 select_maximum_fusion.4
  98.1 0.4 fusion.245
  98.6 0.9 pad.17
  99.5 3.0 %reshape.24 = bf16[16,6,10,1,8,33]{5,4,0,2,1,3:T(8,128)(2,1)S(1)} reshape(bf16[16,6,10,1,264]{4,0,2,1,3:T(8,128)(2,1)} %pad.17) | data formatting | bytes 1013760 | tf_op jit(solution)/shard_map/conv_general_dilated | solution.py:34
  102.5 4.8 %copy.94 = bf16[16,6,10,1,8,33]{0,4,5,2,1,3:T(8,128)(2,1)} copy(bf16[16,6,10,1,8,33]{5,4,0,2,1,3:T(8,128)(2,1)S(1)} %reshape.24) | data formatting | bytes 1013760 | tf_op jit(solution)/shard_map/conv_general_dilated | solution.py:34
  107.4 1.0 slice.312
  108.4 9.4 %broadcast_select_fusion = f32[4,8,8,33,32]{4,2,3,1,0:T(8,128)} fusion(pred[8,33]{0,1:T(8,128)(4,1)S(1)} %copy-done.14, bf16[32,16,3,3,3]{0,1,4,3,2:T(8,128)(2,1)S(1)} %copy.95, bf16[16,6,10,1,7,2]{0,4,5,2,1,3:T(8,128)(2,1)S(1)} %slice.312, bf16[16,6,10,1,8,33]{0,4,5,2,1,3:T(8,128)(2,1)} %copy.94), kind=kOutput, calls=%fused_computation.23 | convolution fusion | flops 235453440 | bytes 1643016 | tf_op jit(solution)/shard_map/conv_general_dilated | solution.py:34
  117.8 5.8 %copy.96 = f32[4,8,8,33,32]{3,2,4,1,0:T(8,128)} copy(f32[4,8,8,33,32]{4,2,3,1,0:T(8,128)} %broadcast_select_fusion) | data formatting | bytes 2162688 | tf_op jit(solution)/shard_map/conv_general_dilated | solution.py:34
  123.6 3.5 %reshape.28 = f32[4,8,1,264,32]{3,4,1,0,2:T(8,128)S(1)} reshape(f32[4,8,8,33,32]{3,2,4,1,0:T(8,128)} %copy.96) | data formatting | bytes 2162688 | tf_op jit(solution)/shard_map/conv_general_dilated | solution.py:34
  127.1 1.5 fusion.96
  128.6 1.3 collective-permute-start.9
  129.9 4.6 %collective-permute-start.8 = (bf16[32,1,8,256]{3,0,2,1:T(8,128)(2,1)S(1)}, bf16[32,1,8,256]{3,0,2,1:T(8,128)(2,1)S(1)}, u32[]{:S(2)}, u32[]{:S(2)}) collective-permute-start(bf16[32,1,8,256]{3,0,2,1:T(8,128)(2,1)S(1)} %get-tuple-element.18), channel_id=1, source_target_pairs={{0,4},{4,8},{8,12},{12,16},{16,20},{20,24},{24,28},{1,5},{5,9},{9,... | collective-permute-start | bytes 393224 | tf_op jit(solution)/shard_map/ppermute | solution.py:24
  134.5 0.4 select_maximum_fusion.2
  135.5 0.3 fusion.64
  136.3 0.3 fusion.61
  137.1 0.3 fusion.58
  138.0 0.3 fusion.55
  138.8 0.3 fusion.52
  139.7 0.3 fusion.49
  140.5 0.3 fusion.46
  141.4 0.3 fusion.43
  142.3 1.3 collective-permute-start.11
  143.6 3.4 %collective-permute-start.10 = (bf16[32,6,1,256]{3,0,2,1:T(8,128)(2,1)S(1)}, bf16[32,6,1,256]{3,0,2,1:T(8,128)(2,1)S(1)}, u32[]{:S(2)}, u32[]{:S(2)}) collective-permute-start(bf16[32,6,1,256]{3,0,2,1:T(8,128)(2,1)S(1)} %get-tuple-element.16), channel_id=1, source_target_pairs={{0,1},{1,2},{2,3},{4,5},{5,6},{6,7},{8,9},{9,10},{10,11},{12,13},{... | collective-permute-start | bytes 294920 | tf_op jit(solution)/shard_map/ppermute | solution.py:24
  147.0 0.3 fusion.40
  147.3 1.1 copy.107
  148.9 0.9 fusion.33
  150.0 4.7 %reshape.31 = bf16[32,6,10,1,8,33]{5,4,0,2,1,3:T(8,128)(2,1)} reshape(bf16[32,6,10,1,264]{4,0,2,1,3:T(8,128)(2,1)S(1)} %pad.19) | data formatting | bytes 2027520 | tf_op jit(solution)/shard_map/conv_general_dilated | solution.py:34
  154.6 7.6 %copy.99 = bf16[32,6,10,1,8,33]{0,4,5,2,1,3:T(8,128)(2,1)} copy(bf16[32,6,10,1,8,33]{5,4,0,2,1,3:T(8,128)(2,1)} %reshape.31) | data formatting | bytes 2027520 | tf_op jit(solution)/shard_map/conv_general_dilated | solution.py:34
  162.2 1.0 slice.316
  163.2 9.7 %broadcast_select_fusion.1 = f32[4,8,8,33,16]{4,2,3,1,0:T(8,128)} fusion(pred[8,33]{0,1:T(8,128)(4,1)S(1)} %copy-done.15, bf16[32,16,3,3,3]{0,1,4,3,2:T(8,128)(2,1)S(1)} %copy-done.3, bf16[32,6,10,1,7,2]{0,4,5,2,1,3:T(8,128)(2,1)S(1)} %slice.316, bf16[32,6,10,1,8,33]{0,4,5,2,1,3:T(8,128)(2,1)} %copy.99), kind=kOutput, calls=%fused_computation.24 | convolution fusion | flops 236931072 | bytes 1636104 | tf_op jit(solution)/shard_map/conv_general_dilated | solution.py:34
  172.9 4.2 %copy.101 = f32[4,8,8,33,16]{3,2,4,1,0:T(8,128)S(1)} copy(f32[4,8,8,33,16]{4,2,3,1,0:T(8,128)} %broadcast_select_fusion.1) | data formatting | bytes 1081344 | tf_op jit(solution)/shard_map/conv_general_dilated | solution.py:34
  177.1 1.5 reshape.35
  178.7 1.1 fusion.104
  180.9 0.3 fusion.88
  181.6 0.3 fusion.85
  183.0 0.3 fusion.79
  186.2 40.3 %all-reduce.5 = (f32[1728]{0:T(1024)S(1)}, f32[13824]{0:T(1024)S(1)}) all-reduce(f32[1728]{0:T(1024)S(1)} %reshape.10, f32[13824]{0:T(1024)S(1)} %reshape.14), channel_id=1, replica_groups=mesh['space'=8,'samp'=4] {'space','samp'}, use_global_device_ids=true, to_apply=%region_0.1 | all-reduce | flops 15552 | bytes 124416 | tf_op jit(solution)/shard_map/psum | solution.py:105
  226.5 0.7 dynamic-slice_multiply_fusion.1
  227.2 0.7 dynamic-slice_multiply_fusion
  (106 shorter events, 12.0 us)
Async XLA Ops:
  1.5 6.3 %collective-permute-start = (bf16[4,1,8,256]{3,0,2,1:T(4,128)(2,1)S(1)}, bf16[4,1,8,256]{3,0,2,1:T(4,128)(2,1)S(1)}, u32[]{:S(2)}, u32[]{:S(2)}) collective-permute-start(bf16[4,1,8,256]{3,0,2,1:T(4,128)(2,1)S(1)} %get-tuple-element.29), channel_id=1, source_target_pairs={{0,4},{4,8},{8,12},{12,16},{16,20},{20,24},{24,28},{1,5},{5,9},{9,... | collective-permute-start | bytes 49160 | tf_op jit(solution)/shard_map/ppermute | solution.py:24
  6.4 5.6 %collective-permute-start.1 = (bf16[4,1,8,256]{3,0,2,1:T(4,128)(2,1)S(1)}, bf16[4,1,8,256]{3,0,2,1:T(4,128)(2,1)S(1)}, u32[]{:S(2)}, u32[]{:S(2)}) collective-permute-start(bf16[4,1,8,256]{3,0,2,1:T(4,128)(2,1)S(1)} %get-tuple-element.28), channel_id=1, source_target_pairs={{4,0},{8,4},{12,8},{16,12},{20,16},{24,20},{28,24},{5,1},{9,5},{13... | collective-permute-start | bytes 49160 | tf_op jit(solution)/shard_map/ppermute | solution.py:26
  7.9 18.2 %copy-start.9 = (bf16[4,1,8,256]{3,0,2,1:T(4,128)(2,1)}, bf16[4,1,8,256]{3,0,2,1:T(4,128)(2,1)S(1)}, u32[]{:S(2)}) copy-start(bf16[4,1,8,256]{3,0,2,1:T(4,128)(2,1)S(1)} %collective-permute-done) | copy-start | bytes 49156
  12.1 1.3 copy-start.7
  12.1 14.6 %collective-permute-start.3 = (bf16[4,6,1,256]{3,0,2,1:T(4,128)(2,1)S(1)}, bf16[4,6,1,256]{3,0,2,1:T(4,128)(2,1)S(1)}, u32[]{:S(2)}, u32[]{:S(2)}) collective-permute-start(bf16[4,6,1,256]{3,0,2,1:T(4,128)(2,1)S(1)} %get-tuple-element.27), channel_id=1, source_target_pairs={{1,0},{2,1},{3,2},{5,4},{6,5},{7,6},{9,8},{10,9},{11,10},{13,12},{... | collective-permute-start | bytes 36872 | tf_op jit(solution)/shard_map/ppermute | solution.py:26
  13.4 13.3 %collective-permute-start.2 = (bf16[4,6,1,256]{3,0,2,1:T(4,128)(2,1)S(1)}, bf16[4,6,1,256]{3,0,2,1:T(4,128)(2,1)S(1)}, u32[]{:S(2)}, u32[]{:S(2)}) collective-permute-start(bf16[4,6,1,256]{3,0,2,1:T(4,128)(2,1)S(1)} %get-tuple-element.26), channel_id=1, source_target_pairs={{0,1},{1,2},{2,3},{4,5},{5,6},{6,7},{8,9},{9,10},{10,11},{12,13},{... | collective-permute-start | bytes 36872 | tf_op jit(solution)/shard_map/ppermute | solution.py:24
  26.3 3.0 %copy-start.13 = (pred[8,33]{0,1:T(8,128)(4,1)S(1)}, pred[8,33]{0,1:T(8,128)(4,1)}, u32[]{:S(2)}) copy-start(pred[8,33]{0,1:T(8,128)(4,1)} %constant.51) | copy-start | bytes 796
  26.7 13.4 %copy-start.4 = (bf16[4,6,1,256]{3,0,2,1:T(4,128)(2,1)}, bf16[4,6,1,256]{3,0,2,1:T(4,128)(2,1)S(1)}, u32[]{:S(2)}) copy-start(bf16[4,6,1,256]{3,0,2,1:T(4,128)(2,1)S(1)} %collective-permute-done.2) | copy-start | bytes 36868
  44.3 7.0 %copy-start.12 = (u32[32]{0:T(128)S(1)}, u32[32]{0:T(128)}, u32[]{:S(2)}) copy-start(u32[32]{0:T(128)} %constant.61) | copy-start | bytes 388
  44.3 8.3 %copy-start.11 = (bf16[1728]{0:T(1024)(128)(2,1)S(1)}, bf16[1728]{0:T(1024)(128)(2,1)}, u32[]{:S(2)}) copy-start(bf16[1728]{0:T(1024)(128)(2,1)} %param.6) | copy-start | bytes 10372
  45.0 52.3 %copy-start.5 = (bf16[4,6,1,256]{3,0,2,1:T(4,128)(2,1)S(1)}, bf16[4,6,1,256]{3,0,2,1:T(4,128)(2,1)}, u32[]{:S(2)}) copy-start(bf16[4,6,1,256]{3,0,2,1:T(4,128)(2,1)} %copy-done.4) | copy-start | bytes 36868
  45.0 47.7 %collective-permute-start.5 = (bf16[16,1,8,256]{3,0,2,1:T(8,128)(2,1)S(1)}, bf16[16,1,8,256]{3,0,2,1:T(8,128)(2,1)S(1)}, u32[]{:S(2)}, u32[]{:S(2)}) collective-permute-start(bf16[16,1,8,256]{3,0,2,1:T(8,128)(2,1)S(1)} %get-tuple-element.25), channel_id=1, source_target_pairs={{4,0},{8,4},{12,8},{16,12},{20,16},{24,20},{28,24},{5,1},{9,5},{13... | collective-permute-start | bytes 196616 | tf_op jit(solution)/shard_map/ppermute | solution.py:26
  46.3 46.4 %collective-permute-start.4 = (bf16[16,1,8,256]{3,0,2,1:T(8,128)(2,1)S(1)}, bf16[16,1,8,256]{3,0,2,1:T(8,128)(2,1)S(1)}, u32[]{:S(2)}, u32[]{:S(2)}) collective-permute-start(bf16[16,1,8,256]{3,0,2,1:T(8,128)(2,1)S(1)} %get-tuple-element.24), channel_id=1, source_target_pairs={{0,4},{4,8},{8,12},{12,16},{16,20},{20,24},{24,28},{1,5},{5,9},{9,... | collective-permute-start | bytes 196616 | tf_op jit(solution)/shard_map/ppermute | solution.py:24
  92.7 15.7 %copy-start.2 = (bf16[32,16,3,3,3]{0,1,4,3,2:T(8,128)(2,1)}, bf16[32,16,3,3,3]{0,1,4,3,2:T(8,128)(2,1)S(1)}, u32[]{:S(2)}) copy-start(bf16[32,16,3,3,3]{0,1,4,3,2:T(8,128)(2,1)S(1)} %copy.95) | copy-start | bytes 82948
  92.8 5.4 %collective-permute-start.7 = (bf16[16,6,1,256]{3,0,2,1:T(8,128)(2,1)S(1)}, bf16[16,6,1,256]{3,0,2,1:T(8,128)(2,1)S(1)}, u32[]{:S(2)}, u32[]{:S(2)}) collective-permute-start(bf16[16,6,1,256]{3,0,2,1:T(8,128)(2,1)S(1)} %get-tuple-element.23), channel_id=1, source_target_pairs={{1,0},{2,1},{3,2},{5,4},{6,5},{7,6},{9,8},{10,9},{11,10},{13,12},{... | collective-permute-start | bytes 147464 | tf_op jit(solution)/shard_map/ppermute | solution.py:26
  94.1 4.1 %collective-permute-start.6 = (bf16[16,6,1,256]{3,0,2,1:T(8,128)(2,1)S(1)}, bf16[16,6,1,256]{3,0,2,1:T(8,128)(2,1)S(1)}, u32[]{:S(2)}, u32[]{:S(2)}) collective-permute-start(bf16[16,6,1,256]{3,0,2,1:T(8,128)(2,1)S(1)} %get-tuple-element.22), channel_id=1, source_target_pairs={{0,1},{1,2},{2,3},{4,5},{5,6},{6,7},{8,9},{9,10},{10,11},{12,13},{... | collective-permute-start | bytes 147464 | tf_op jit(solution)/shard_map/ppermute | solution.py:24
  102.5 5.9 %copy-start.14 = (pred[8,33]{0,1:T(8,128)(4,1)S(1)}, pred[8,33]{0,1:T(8,128)(4,1)}, u32[]{:S(2)}) copy-start(pred[8,33]{0,1:T(8,128)(4,1)} %constant.51) | copy-start | bytes 796
  128.6 13.6 %collective-permute-start.9 = (bf16[32,1,8,256]{3,0,2,1:T(8,128)(2,1)S(1)}, bf16[32,1,8,256]{3,0,2,1:T(8,128)(2,1)S(1)}, u32[]{:S(2)}, u32[]{:S(2)}) collective-permute-start(bf16[32,1,8,256]{3,0,2,1:T(8,128)(2,1)S(1)} %get-tuple-element.19), channel_id=1, source_target_pairs={{4,0},{8,4},{12,8},{16,12},{20,16},{24,20},{28,24},{5,1},{9,5},{13... | collective-permute-start | bytes 393224 | tf_op jit(solution)/shard_map/ppermute | solution.py:26
  129.9 12.3 %collective-permute-start.8 = (bf16[32,1,8,256]{3,0,2,1:T(8,128)(2,1)S(1)}, bf16[32,1,8,256]{3,0,2,1:T(8,128)(2,1)S(1)}, u32[]{:S(2)}, u32[]{:S(2)}) collective-permute-start(bf16[32,1,8,256]{3,0,2,1:T(8,128)(2,1)S(1)} %get-tuple-element.18), channel_id=1, source_target_pairs={{0,4},{4,8},{8,12},{12,16},{16,20},{20,24},{24,28},{1,5},{5,9},{9,... | collective-permute-start | bytes 393224 | tf_op jit(solution)/shard_map/ppermute | solution.py:24
  142.3 6.6 %collective-permute-start.11 = (bf16[32,6,1,256]{3,0,2,1:T(8,128)(2,1)S(1)}, bf16[32,6,1,256]{3,0,2,1:T(8,128)(2,1)S(1)}, u32[]{:S(2)}, u32[]{:S(2)}) collective-permute-start(bf16[32,6,1,256]{3,0,2,1:T(8,128)(2,1)S(1)} %get-tuple-element.17), channel_id=1, source_target_pairs={{1,0},{2,1},{3,2},{5,4},{6,5},{7,6},{9,8},{10,9},{11,10},{13,12},{... | collective-permute-start | bytes 294920 | tf_op jit(solution)/shard_map/ppermute | solution.py:26
  143.6 5.3 %collective-permute-start.10 = (bf16[32,6,1,256]{3,0,2,1:T(8,128)(2,1)S(1)}, bf16[32,6,1,256]{3,0,2,1:T(8,128)(2,1)S(1)}, u32[]{:S(2)}, u32[]{:S(2)}) collective-permute-start(bf16[32,6,1,256]{3,0,2,1:T(8,128)(2,1)S(1)} %get-tuple-element.16), channel_id=1, source_target_pairs={{0,1},{1,2},{2,3},{4,5},{5,6},{6,7},{8,9},{9,10},{10,11},{12,13},{... | collective-permute-start | bytes 294920 | tf_op jit(solution)/shard_map/ppermute | solution.py:24
  154.6 8.6 %copy-start.3 = (bf16[32,16,3,3,3]{0,1,4,3,2:T(8,128)(2,1)S(1)}, bf16[32,16,3,3,3]{0,1,4,3,2:T(8,128)(2,1)}, u32[]{:S(2)}) copy-start(bf16[32,16,3,3,3]{0,1,4,3,2:T(8,128)(2,1)} %copy-done.2) | copy-start | bytes 82948
  154.6 8.6 %copy-start.15 = (pred[8,33]{0,1:T(8,128)(4,1)S(1)}, pred[8,33]{0,1:T(8,128)(4,1)}, u32[]{:S(2)}) copy-start(pred[8,33]{0,1:T(8,128)(4,1)} %constant.51) | copy-start | bytes 796
  177.1 2.7 %copy-start.1 = (bf16[4,6,10,258]{3,0,2,1:T(4,128)(2,1)S(1)}, bf16[4,6,10,258]{3,0,2,1:T(4,128)(2,1)}, u32[]{:S(2)}) copy-start(bf16[4,6,10,258]{3,0,2,1:T(4,128)(2,1)} %select_maximum_fusion.4) | copy-start | bytes 371524
  177.1 2.9 %copy-start.6 = (bf16[4,6,1,256]{3,0,2,1:T(4,128)(2,1)S(1)}, bf16[4,6,1,256]{3,0,2,1:T(4,128)(2,1)}, u32[]{:S(2)}) copy-start(bf16[4,6,1,256]{3,0,2,1:T(4,128)(2,1)} %copy-done.4) | copy-start | bytes 36868
  178.7 2.0 copy-start.10
  180.5 2.3 copy-start
  182.3 2.5 %copy-start.8 = (bf16[4,1,8,256]{3,0,2,1:T(4,128)(2,1)S(1)}, bf16[4,1,8,256]{3,0,2,1:T(4,128)(2,1)}, u32[]{:S(2)}) copy-start(bf16[4,1,8,256]{3,0,2,1:T(4,128)(2,1)} %copy-done.7) | copy-start | bytes 49156
where the time goes:
time: 230 us; the launch traced here: 228 us
  blocking collectives  83.2 us (36%)
  local copies, waits for them, and re-layouts  56.7 us (25%)
  matrix products  43.4 us (19%)
  starting transfers between devices  31.8 us (14%)
  other arithmetic  6.9 us (3%)
  waiting for transfers between devices  3.44 us (1%)
  between operations  2.53 us (1%)
    conv_general_dilated x15, local copies, waits for them, and re-layouts, conv_valid(): lax.conv_general_dilated(padded[None], kernel, (1, 1, 1), 'VALID', dimens...  44.3 us
    unnamed x2, blocking collectives  42.9 us
    psum x1, blocking collectives, on_device(): total_one, total_two = lax.psum((term_one, term_two), ('space', 'samp'))  40.3 us
    conv_general_dilated x3, matrix products, conv_valid(): lax.conv_general_dilated(padded[None], kernel, (1, 1, 1), 'VALID', dimens...  29.7 us
    ppermute x6, starting transfers between devices, with_halo(): lax.ppermute(tail, axis, [(i, (i + 1) % count) for i in range(ends)])  24.1 us
    dot_general x54, matrix products, kernel_grad(): lax.dot_general(flat_out, window, (((1,), (1,)), ((), ())), preferred_ele...  13.7 us
    ppermute x6, starting transfers between devices, with_halo(): lax.ppermute(head, axis, [((i + 1) % count, i) for i in range(ends)])  7.75 us
    unnamed x42, local copies, waits for them, and re-layouts  6 us
  transfers between devices with their start and end apart: 12, of which 2 were waited for; matrix products, arithmetic and copies ran while one was open for 8% of the time, Pallas kernels for 0%

commit v1 on v0

v1 whole, which is shorter than its diff:
```python
import functools
import math

import jax
import jax.numpy as jnp
from jax import lax
from jax.experimental import pallas as pl
from jax.experimental.pallas import tpu as pltpu
from jax.sharding import PartitionSpec as P

CIN = 4
C1 = 16
C2 = 32
SLOPE = 0.3
MESH = pl.DeviceIdType.MESH
F32 = jnp.float32
BF16 = jnp.bfloat16
DIRS = [(dx, dy) for dx in (-1, 0, 1) for dy in (-1, 0, 1) if (dx, dy) != (0, 0)]


def spans(delta, size, width):
    if delta == 1:
        return (size - width, width), (0, width)
    if delta == -1:
        return (0, width), (size + width, width)
    return (0, size), (width, size)


def leaky(values):
    return jnp.where(values > 0, values, SLOPE * values)


def exchange_kernel(
    n_space, n_samp, v_ref, c_ref, f1_ref, f2_ref, vp_ref, cp_ref, g1_ref, g2_ref,
    send_v, recv_v, send_c, recv_c, send_1, recv_1, send_2, recv_2,
):
    s = lax.axis_index("space")
    m = lax.axis_index("samp")
    size_x, size_y = v_ref.shape[0], v_ref.shape[1]

    vp_ref[...] = jnp.zeros_like(vp_ref)

    def zero_row(x, carry):
        cp_ref[x] = jnp.zeros(cp_ref.shape[1:], cp_ref.dtype)
        return carry

    lax.fori_loop(0, cp_ref.shape[0], zero_row, 0)

    def there(dx, dy):
        return (s + dx >= 0) & (s + dx < n_space) & (m + dy >= 0) & (m + dy < n_samp)

    barrier = pltpu.get_barrier_semaphore()
    peers = n_samp - 1 + n_space - 1
    for dx, dy in DIRS:
        if dx == 0 or dy == 0:
            continue
        peers = peers + jnp.where(there(dx, dy), 1, 0)

        @pl.when(there(dx, dy))
        def _():
            pl.semaphore_signal(barrier, inc=1, device_id=(s + dx, m + dy), device_id_type=MESH)
    for k in range(1, n_samp):
        pl.semaphore_signal(barrier, inc=1, device_id=(s, lax.rem(m + k, n_samp)), device_id_type=MESH)

    def greet(k, carry):
        pl.semaphore_signal(barrier, inc=1, device_id=(lax.rem(s + k, n_space), m), device_id_type=MESH)
        return carry

    lax.fori_loop(1, n_space, greet, 0)
    pl.semaphore_wait(barrier, peers)

    def copy_1(k):
        return pltpu.make_async_remote_copy(
            src_ref=f1_ref, dst_ref=g1_ref.at[m], send_sem=send_1.at[k], recv_sem=recv_1.at[k],
            device_id=(s, lax.rem(m + k, n_samp)), device_id_type=MESH)

    def copy_2(k):
        return pltpu.make_async_remote_copy(
            src_ref=f2_ref, dst_ref=g2_ref.at[s], send_sem=send_2.at[k], recv_sem=recv_2.at[k],
            device_id=(lax.rem(s + k, n_space), m), device_id_type=MESH)

    def halo(src, dst, width, send, recv, slot, dx, dy):
        (sx, nx), (tx, _) = spans(dx, size_x, width)
        (sy, ny), (ty, _) = spans(dy, size_y, width)
        return pltpu.make_async_remote_copy(
            src_ref=src.at[pl.ds(sx, nx), pl.ds(sy, ny)], dst_ref=dst.at[pl.ds(tx, nx), pl.ds(ty, ny)],
            send_sem=send.at[slot], recv_sem=recv.at[slot],
            device_id=(jnp.clip(s + dx, 0, n_space - 1), jnp.clip(m + dy, 0, n_samp - 1)),
            device_id_type=MESH)

    vol = [halo(v_ref, vp_ref, 3, send_v, recv_v, j, dx, dy) for j, (dx, dy) in enumerate(DIRS)]
    cot = [halo(c_ref, cp_ref, 1, send_c, recv_c, j, dx, dy) for j, (dx, dy) in enumerate(DIRS)]
    for k in range(1, n_samp):
        copy_1(k).start()

    def start_2(k, carry):
        copy_2(k).start()
        return carry

    lax.fori_loop(1, n_space, start_2, 0)
    for group in (vol, cot):
        for copy, (dx, dy) in zip(group, DIRS):
            @pl.when(there(dx, dy))
            def _():
                copy.start()

    g1_ref[m] = f1_ref[...]
    g2_ref[s] = f2_ref[...]
    vp_ref[3 : 3 + size_x, 3 : 3 + size_y] = v_ref[...]

    def centre(x, carry):
        cp_ref[x + 1, 1 : 1 + size_y] = c_ref[x]
        return carry

    lax.fori_loop(0, size_x, centre, 0)

    for k in range(1, n_samp):
        copy_1(k).wait()

    def wait_2(k, carry):
        copy_2(k).wait()
        return carry

    lax.fori_loop(1, n_space, wait_2, 0)
    for group in (vol, cot):
        for copy, (dx, dy) in zip(group, DIRS):
            @pl.when(there(-dx, -dy))
            def _():
                copy.wait_recv()

            @pl.when(there(dx, dy))
            def _():
                copy.wait_send()


def tap_sum(t, rows, lane, last):
    low = jnp.where(lane == 0, 0.0, pltpu.roll(t[:rows], 1, axis=1))
    high = jnp.where(lane == last, 0.0, pltpu.roll(t[2 * rows :], last, axis=1))
    return t[rows : 2 * rows] + low + high


def tap_spread(b, lane, last):
    low = jnp.where(lane == last, 0.0, pltpu.roll(b, last, axis=1))
    high = jnp.where(lane == 0, 0.0, pltpu.roll(b, 1, axis=1))
    return jnp.concatenate([low, b, high], axis=0)


def dot(a, b):
    return lax.dot_general(a, b, (((1,), (0,)), ((), ())), preferred_element_type=F32)


def dot_nt(a, b):
    return lax.dot_general(a, b, (((1,), (1,)), ((), ())), preferred_element_type=F32)


def compute_kernel(
    n_space, n_samp, v_ref, c_ref, w1_ref, w2_ref, w3_ref, act_ref, o1_ref, o2_ref,
    a1, a2, a3, hid, back, pre, t1, perm, acc1, acc2, act,
):
    s = lax.axis_index("space")
    m = lax.axis_index("samp")
    size_z = v_ref.shape[-1]
    last = size_z - 1
    size_x, size_y = act_ref.shape[1], act_ref.shape[2]
    high_y = size_y + 4

    def lanes(rows):
        return lax.broadcasted_iota(jnp.int32, (rows, size_z), 1)

    lane1 = lanes(C1)
    lane2 = lanes(C2)
    base1 = w1_ref[...]
    for y in range(high_y):
        row = base1 if y == 0 else pltpu.roll(base1, 4 * y, axis=1)
        a1[48 * y : 48 * y + 48] = row[:, :192].astype(BF16)
    base2 = w2_ref[...]
    a2[:96] = base2[:, :192].astype(BF16)
    a2[96:] = pltpu.roll(base2, 16, axis=1)[:, :192].astype(BF16)
    base3 = w3_ref[...]
    a3[:48] = base3.astype(BF16)
    a3[48:] = pltpu.roll(base3, 32, axis=1).astype(BF16)
    r = lax.broadcasted_iota(jnp.int32, (C2 * size_y, C2 * size_y), 0)
    q = lax.broadcasted_iota(jnp.int32, (C2 * size_y, C2 * size_y), 1)
    from_row = (r % size_y) * C2 + r // size_y
    perm[...] = jnp.where(q == from_row, 1.0, 0.0).astype(BF16)
    acc1[...] = jnp.zeros_like(acc1)
    acc2[...] = jnp.zeros_like(acc2)

    def vwin(x):
        return jnp.concatenate([v_ref[x], v_ref[x + 1], v_ref[x + 2]], axis=0)

    def layer1(x, carry):
        gx = s * size_x + x - 2
        ok_x = (gx >= 0) & (gx < n_space * size_x)
        t1[...] = dot(a1[...], vwin(x))
        for y in range(high_y):
            gy = m * size_y + y - 2
            ok = ok_x & (gy >= 0) & (gy < n_samp * size_y)
            p = tap_sum(t1[48 * y : 48 * y + 48], C1, lane1, last)
            pre[x, 16 * y : 16 * y + 16] = p
            h = leaky(p) * jnp.where(ok, 1.0, 0.0)
            hid[x, 16 * y : 16 * y + 16] = h.astype(BF16)
        return carry

    lax.fori_loop(0, size_x + 4, layer1, 0)

    def hwin(x, y):
        return jnp.concatenate([hid[x + k, 16 * y : 16 * y + 64] for k in range(3)], axis=0)

    def layer2(x, carry):
        for y in range(0, size_y + 2, 2):
            t = dot(a2[...], hwin(x, y))
            for half in range(2):
                p = tap_sum(t[96 * half : 96 * half + 96], C2, lane2, last)
                rows = slice(C2 * (y + half), C2 * (y + half) + C2)
                act[x, rows] = leaky(p).astype(BF16)
                b = c_ref[x, y + half].astype(F32) * jnp.where(p > 0, 1.0, SLOPE)
                back[x, rows] = b.astype(BF16)
        return carry

    lax.fori_loop(0, size_x + 2, layer2, 0)

    def finish(x, carry):
        value = dot(perm[...], act[x + 1, C2 : C2 + C2 * size_y])
        act_ref[:, x] = value.reshape(C2, size_y, size_z).astype(BF16)
        pieces = []
        for y in range(0, size_y, 2):
            win = jnp.concatenate([back[x + k, C2 * y : C2 * y + 128] for k in range(3)], axis=0)
            t = dot(a3[...], win)
            both = []
            for half in range(2):
                d = tap_sum(t[48 * half : 48 * half + 48], C1, lane1, last)
                p = pre[x + 2, 16 * (y + half + 2) : 16 * (y + half + 2) + 16]
                b1 = d * jnp.where(p > 0, 1.0, SLOPE)
                b1 = b1.astype(BF16).astype(F32)
                pieces.append(tap_spread(b1, lane1, last).astype(BF16))
                start = C2 * (y + half + 1)
                b2 = back[x + 1, start : start + C2].astype(F32)
                both.append(tap_spread(b2, lane2, last).astype(BF16))
            acc2[...] += dot_nt(jnp.concatenate(both, axis=0), hwin(x + 1, y + 1))
        acc1[...] += dot_nt(jnp.concatenate(pieces, axis=0), vwin(x + 2))
        return carry

    lax.fori_loop(0, size_x, finish, 0)

    def wide(values, rows):
        return jnp.concatenate([values, jnp.zeros((rows, 64), F32)], axis=1)

    o2_ref[...] = wide(acc2[:96], 96) + pltpu.roll(wide(acc2[96:], 96), 256 - 16, axis=1)
    total = jnp.zeros((48, 256), F32)
    for y in range(size_y):
        total = total + pltpu.roll(wide(acc1[48 * y : 48 * y + 48], 48), 256 - 4 * (y + 2), axis=1)
    o1_ref[...] = total


def reduce_kernel(
    n_space, n_samp, scale, g1_ref, g2_ref, o1_ref, o2_ref,
    part1, part2, full1, full2, mine1, mine2, send_a1, recv_a1, send_a2, recv_a2, send_b1, recv_b1, send_b2, recv_b2,
):
    s = lax.axis_index("space")
    m = lax.axis_index("samp")
    barrier = pltpu.get_barrier_semaphore()

    def samp_peer(k):
        return lax.rem(m + k, n_samp)

    def space_peer(k):
        return lax.rem(s + k, n_space)

    for k in range(1, n_samp):
        pl.semaphore_signal(barrier, inc=1, device_id=(s, samp_peer(k)), device_id_type=MESH)

    def over_space(body):
        def step(k, carry):
            body(k)
            return carry

        lax.fori_loop(1, n_space, step, 0)

    over_space(lambda k: pl.semaphore_signal(
        barrier, inc=1, device_id=(space_peer(k), m), device_id_type=MESH))
    pl.semaphore_wait(barrier, n_samp - 1 + n_space - 1)

    def first_1(k):
        return pltpu.make_async_remote_copy(
            src_ref=g1_ref.at[samp_peer(k)], dst_ref=part1.at[m], send_sem=send_a1.at[k],
            recv_sem=recv_a1.at[k], device_id=(s, samp_peer(k)), device_id_type=MESH)

    def first_2(k):
        return pltpu.make_async_remote_copy(
            src_ref=g2_ref.at[space_peer(k)], dst_ref=part2.at[s], send_sem=send_a2.at[k],
            recv_sem=recv_a2.at[k], device_id=(space_peer(k), m), device_id_type=MESH)

    def second_1(k):
        return pltpu.make_async_remote_copy(
            src_ref=mine1, dst_ref=full1.at[s], send_sem=send_b1.at[k],
            recv_sem=recv_b1.at[k], device_id=(space_peer(k), m), device_id_type=MESH)

    def second_2(k):
        return pltpu.make_async_remote_copy(
            src_ref=mine2, dst_ref=full2.at[m], send_sem=send_b2.at[k],
            recv_sem=recv_b2.at[k], device_id=(s, samp_peer(k)), device_id_type=MESH)

    over_space(lambda k: first_2(k).start())
    for k in range(1, n_samp):
        first_1(k).start()
    part1[m] = g1_ref[m]
    part2[s] = g2_ref[s]
    for k in range(1, n_samp):
        first_1(k).wait()
    mine1[...] = jnp.sum(part1[...], axis=0)
    over_space(lambda k: second_1(k).start())
    over_space(lambda k: first_2(k).wait())
    mine2[...] = jnp.sum(part2[...], axis=0)
    for k in range(1, n_samp):
        second_2(k).start()
    full1[s] = mine1[...]
    full2[m] = mine2[...]
    over_space(lambda k: second_1(k).wait())
    for k in range(1, n_samp):
        second_2(k).wait()
    o1_ref[...] = jnp.sum(full1[...], axis=0) * scale
    o2_ref[...] = jnp.sum(full2[...], axis=0) * scale


VMEM = pl.BlockSpec(memory_space=pltpu.VMEM)


def on_device(n_space, n_samp, volume, filters_one, filters_two, cotangent):
    _, size_x, size_y, size_z = volume.shape
    len1 = filters_one.shape[0]
    len2 = filters_two.shape[0]
    sem = pltpu.SemaphoreType.DMA
    v_rows = volume.transpose(1, 2, 0, 3)
    c_rows = cotangent.transpose(1, 2, 0, 3)
    vp, cp, all1, all2 = pl.pallas_call(
        functools.partial(exchange_kernel, n_space, n_samp),
        out_shape=[
            jax.ShapeDtypeStruct((size_x + 6, size_y + 8, CIN, size_z), BF16),
            jax.ShapeDtypeStruct((size_x + 2, size_y + 2, C2, size_z), BF16),
            jax.ShapeDtypeStruct((n_samp, 1, len1), BF16),
            jax.ShapeDtypeStruct((n_space, 1, len2), BF16),
        ],
        in_specs=[VMEM] * 4,
        out_specs=[VMEM] * 4,
        scratch_shapes=[
            sem((8,)), sem((8,)), sem((8,)), sem((8,)),
            sem((n_samp,)), sem((n_samp,)), sem((n_space,)), sem((n_space,)),
        ],
        compiler_params=pltpu.CompilerParams(
            collective_id=0, has_side_effects=True, vmem_limit_bytes=40 * 2**20),
    )(v_rows, c_rows, filters_one.reshape(1, len1), filters_two.reshape(1, len2))

    kern1 = all1.reshape(C1, CIN, 3, 3, 3).astype(F32)
    kern2 = all2.reshape(C2, C1, 3, 3, 3).astype(F32)
    base1 = kern1.transpose(4, 0, 2, 3, 1).reshape(3 * C1, 3, 3 * CIN)
    base1 = jnp.pad(base1, ((0, 0), (0, 0), (0, 64 - 3 * CIN))).reshape(3 * C1, 192)
    base1 = jnp.pad(base1, ((0, 0), (0, 64)))
    base2 = kern2.transpose(4, 0, 2, 3, 1).reshape(3 * C2, 3, 3 * C1)
    base2 = jnp.pad(base2, ((0, 0), (0, 0), (0, 64 - 3 * C1))).reshape(3 * C2, 192)
    base2 = jnp.pad(base2, ((0, 0), (0, 64)))
    base3 = jnp.flip(kern2, (2, 3, 4)).transpose(4, 1, 2, 3, 0).reshape(3 * C1, 3, 3 * C2)
    base3 = jnp.pad(base3, ((0, 0), (0, 0), (0, 128 - 3 * C2))).reshape(3 * C1, 384)

    high_y = size_y + 4
    activation, grad1, grad2 = pl.pallas_call(
        functools.partial(compute_kernel, n_space, n_samp),
        out_shape=[
            jax.ShapeDtypeStruct((C2, size_x, size_y, size_z), BF16),
            jax.ShapeDtypeStruct((48, 256), F32),
            jax.ShapeDtypeStruct((96, 256), F32),
        ],
        in_specs=[VMEM] * 5,
        out_specs=[VMEM] * 3,
        scratch_shapes=[
            pltpu.VMEM((48 * high_y, 192), BF16),
            pltpu.VMEM((192, 192), BF16),
            pltpu.VMEM((96, 384), BF16),
            pltpu.VMEM((size_x + 4, 16 * high_y, size_z), BF16),
            pltpu.VMEM((size_x + 2, C2 * (size_y + 2), size_z), BF16),
            pltpu.VMEM((size_x + 4, 16 * high_y, size_z), F32),
            pltpu.VMEM((48 * high_y, size_z), F32),
            pltpu.VMEM((C2 * size_y, C2 * size_y), BF16),
            pltpu.VMEM((48 * size_y, 192), F32),
            pltpu.VMEM((192, 192), F32),
            pltpu.VMEM((size_x + 2, C2 * (size_y + 2), size_z), BF16),
        ],
        compiler_params=pltpu.CompilerParams(vmem_limit_bytes=48 * 2**20),
    )(vp.reshape(size_x + 6, CIN * (size_y + 8), size_z), cp, base1, base2, base3)

    grad1 = grad1[:, :192].reshape(3, C1, 3, 64)[..., : 3 * CIN].reshape(3, C1, 3, 3, CIN)
    grad1 = grad1.transpose(1, 4, 2, 3, 0).reshape(n_samp, 1, len1)
    grad2 = grad2[:, :192].reshape(3, C2, 3, 64)[..., : 3 * C1].reshape(3, C2, 3, 3, C1)
    grad2 = grad2.transpose(1, 4, 2, 3, 0).reshape(n_space, 1, len2)
    scale = 1.0 / math.sqrt(float(size_x * n_space * size_y * n_samp * size_z))
    out1, out2 = pl.pallas_call(
        functools.partial(reduce_kernel, n_space, n_samp, scale),
        out_shape=[
            jax.ShapeDtypeStruct((1, len1), F32),
            jax.ShapeDtypeStruct((1, len2), F32),
        ],
        in_specs=[VMEM] * 2,
        out_specs=[VMEM] * 2,
        scratch_shapes=[
            pltpu.VMEM((n_samp, 1, len1), F32),
            pltpu.VMEM((n_space, 1, len2), F32),
            pltpu.VMEM((n_space, 1, len1), F32),
            pltpu.VMEM((n_samp, 1, len2), F32),
            pltpu.VMEM((1, len1), F32),
            pltpu.VMEM((1, len2), F32),
            sem((n_samp,)), sem((n_samp,)), sem((n_space,)), sem((n_space,)),
            sem((n_space,)), sem((n_space,)), sem((n_samp,)), sem((n_samp,)),
        ],
        compiler_params=pltpu.CompilerParams(collective_id=1, has_side_effects=True),
    )(grad1, grad2)
    return activation, out1.reshape(len1), out2.reshape(len2)


def solution(mesh):
    in_specs = (
        P(None, "space", "samp", None),
        P("samp"),
        P("space"),
        P(None, "space", "samp", None),
    )
    out_specs = (P(None, "space", "samp", None), P("samp"), P("space"))
    return jax.shard_map(
        functools.partial(on_device, mesh.shape["space"], mesh.shape["samp"]),
        mesh=mesh, in_specs=in_specs, out_specs=out_specs, check_vma=False,
    )
```

time: 230 us -> 76.7 us (0.33)
  blocking collectives: 83.2 us -> 0 us
  matrix products: 43.4 us -> 0 us
  Pallas kernels: 0 us -> 38.5 us
  starting transfers between devices: 31.8 us -> 0 us
  local copies, waits for them, and re-layouts: 56.7 us -> 35.2 us
  other arithmetic: 6.9 us -> 1.5 us
  waiting for transfers between devices: 3.44 us -> 0 us
    conv_general_dilated x15 -> x0, local copies, waits for them, and re-layouts: 44.3 us -> none  [conv_valid(): lax.conv_general_dilated(padded[None], kernel, (1, 1, 1), 'VALID', dimens...]
    unnamed x2 -> x0, blocking collectives: 42.9 us -> none
    psum x1 -> x0, blocking collectives: 40.3 us -> none  [on_device(): total_one, total_two = lax.psum((term_one, term_two), ('space', 'samp'))]
    pallas_call x0 -> x3, Pallas kernels: none -> 38.5 us  [the longest x1 17.2 us: on_device(): pl.pallas_call(functools.partial(exchange_kernel, n_space, n_samp), out_s...]
    ppermute x12 -> x0, starting transfers between devices: 31.8 us -> none  [the longest x6 24.1 us: with_halo(): lax.ppermute(tail, axis, [(i, (i + 1) % count) for i in range(ends)])]
    conv_general_dilated x3 -> x0, matrix products: 29.7 us -> none  [conv_valid(): lax.conv_general_dilated(padded[None], kernel, (1, 1, 1), 'VALID', dimens...]
    dot_general x54 -> x0, matrix products: 13.7 us -> none  [kernel_grad(): lax.dot_general(flat_out, window, (((1,), (1,)), ((), ())), preferred_ele...]
    rev x0 -> x1, local copies, waits for them, and re-layouts: none -> 10.5 us  [on_device(): jnp.flip(kern2, (2, 3, 4)).transpose(4, 1, 2, 3, 0)]
  transfers between devices with their start and end apart: 12 -> 0, of which waited for: 2 -> 0; matrix products, arithmetic and copies ran while one was open for 8% -> 0% of each run, Pallas kernels for 0% -> 0%
where the time goes in v1:
time: 76.7 us; the launch traced here: 75.9 us
  Pallas kernels  38.5 us (50%)
  local copies, waits for them, and re-layouts  35.2 us (46%)
  other arithmetic  1.5 us (2%)
  between operations  0.8 us (1%)
    pallas_call x1, Pallas kernels, on_device(): pl.pallas_call(functools.partial(exchange_kernel, n_space, n_samp), out_s...  17.2 us
    pallas_call x1, Pallas kernels, on_device(): pl.pallas_call(functools.partial(reduce_kernel, n_space, n_samp, scale),...  12.2 us
    rev x1, local copies, waits for them, and re-layouts, on_device(): jnp.flip(kern2, (2, 3, 4)).transpose(4, 1, 2, 3, 0)  10.5 us
    pallas_call x1, Pallas kernels, on_device(): pl.pallas_call(functools.partial(compute_kernel, n_space, n_samp), out_sh...  9.01 us
    unnamed x6, local copies, waits for them, and re-layouts  7.29 us
    transpose x1, local copies, waits for them, and re-layouts, on_device(): grad2 = grad2.transpose(1, 4, 2, 3, 0).reshape(n_space, 1, len2)  3.54 us
    convert_element_type x1, local copies, waits for them, and re-layouts, on_device(): kern2 = all2.reshape(C2, C1, 3, 3, 3).astype(F32)  3.49 us
    transpose x1, local copies, waits for them, and re-layouts, on_device(): base2 = kern2.transpose(4, 0, 2, 3, 1).reshape(3 * C2, 3, 3 * C1)  3.39 us

profile of v1, /device:TPU:0, one launch (start us, length us, event | category | flops | bytes accessed | tf_op | source)
XLA Modules:
  0.0 75.9 jit_solution(2167814389652260079)
XLA Ops:
  0.6 0.7 reshape.65.f1_ref
  1.3 0.7 reshape.66.f2_ref
  2.0 0.9 %copy.36 = bf16[4,4,8,256]{3,0,2,1:T(4,128)(2,1)S(1)} copy(bf16[4,4,8,256]{3,2,1,0:T(8,128)(2,1)} %param.4) | data formatting | bytes 131072 | tf_op args[0]
  2.9 1.3 %copy.34 = bf16[32,4,8,256]{3,0,2,1:T(8,128)(2,1)S(1)} copy(bf16[32,4,8,256]{3,2,1,0:T(8,128)(2,1)} %param.7) | data formatting | bytes 1048576 | tf_op args[3]
  4.2 17.2 %shard_map.67 = (bf16[10,16,4,256]{3,2,1,0:T(4,128)(2,1)S(1)}, bf16[6,10,32,256]{3,2,1,0:T(8,128)(2,1)S(1)}, bf16[4,1,432]{2,1,0:T(2,128)(2,1)S(1)}, bf16[8,1,1728]{2,1,0:T(2,128)(2,1)S(1)}) custom-call(bf16[4,8,4,256]{3,2,1,0:T(4,128)(2,1)S(1)} %bitcast.32, bf16[4,8,32,256]{3,2,1,0:T(8,128)(2,1)S(1)} %bitcast.30, bf16[1,432]{1,0:T(2,128)(2,1)S(1)} %reshape.65.f1_ref, ...), custom_call_target="tpu_custom_call" | custom-call | tf_op jit(solution)/shard_map/pallas_call | solution.py:336
  21.5 0.1 reshape.67.v_ref
  21.6 0.1 convert_reduce_fusion
  21.7 0.3 convert_element_type.20
  22.0 0.3 copy.14
  22.3 0.1 reshape.68
  22.4 0.1 copy.26
  22.6 3.5 %reshape.82 = f32[32,16,3,3,3]{4,3,2,1,0:T(4,128)} reshape(f32[8,1728]{1,0:T(8,128)S(1)} %convert_reduce_fusion) | data formatting | bytes 110592 | tf_op jit(solution)/shard_map/convert_element_type | solution.py:355
  26.0 3.4 %copy.16 = f32[3,32,3,3,16]{1,0,4,3,2:T(4,128)S(1)} copy(f32[3,32,3,3,16]{0,3,2,4,1:T(4,128)} %bitcast.35) | data formatting | bytes 110592 | tf_op jit(solution)/shard_map/transpose | solution.py:359
  29.4 0.2 reshape.70
  29.6 0.1 copy.17
  29.7 10.5 %rev.4 = f32[32,16,3,3,3]{4,3,2,1,0:T(4,128)} reverse(f32[32,16,3,3,3]{4,3,2,1,0:T(4,128)} %reshape.82), dimensions={2,3,4} | reverse | bytes 110592 | tf_op jit(solution)/shard_map/jit(_flip)/rev | solution.py:362
  40.2 3.6 %copy.28 = f32[3,16,3,3,32]{4,3,2,1,0:T(4,128)S(1)} copy(f32[3,16,3,3,32]{0,3,2,1,4:T(4,128)} %bitcast.36) | data formatting | bytes 110592
  43.8 0.2 reshape.87
  44.0 9.0 %shard_map.68 = (bf16[32,4,8,256]{3,2,1,0:T(8,128)(2,1)}, f32[48,256]{1,0:T(8,128)S(1)}, f32[96,256]{1,0:T(8,128)S(1)}) custom-call(bf16[10,64,256]{2,1,0:T(8,128)(2,1)S(1)} %reshape.67.v_ref, bf16[6,10,32,256]{3,2,1,0:T(8,128)(2,1)S(1)} %get-tuple-element.13.c_ref, f32[48,256]{1,0:T(8,128)S(1)} %pad_convert_fusion.w1_ref, f32[96,256]{1,0:T(8,128)S(1)} %pad.27.w2_ref, ...), custom_call_target="tpu_custom_call" | custom-call | tf_op jit(solution)/shard_map/pallas_call | solution.py:366
  53.1 0.1 reshape.74
  53.1 0.1 copy.20
  53.3 0.1 reshape.77
  53.4 0.1 copy.22
  53.6 0.3 copy.21
  53.9 0.9 %reshape.83.g1_ref = f32[4,1,432]{2,1,0:T(1,128)} reshape(f32[16,4,3,3,3]{4,3,2,1,0:T(4,128)S(1)} %copy.21) | data formatting | bytes 13824 | tf_op jit(solution)/shard_map/reshape | solution.py:392
  54.9 3.5 %copy.23 = f32[32,16,3,3,3]{4,3,2,1,0:T(4,128)S(1)} copy(f32[32,16,3,3,3]{0,1,3,2,4:T(8,128)S(1)} %bitcast.37) | data formatting | bytes 110592 | tf_op jit(solution)/shard_map/transpose | solution.py:394
  58.4 2.7 %reshape.84.g2_ref = f32[8,1,1728]{2,1,0:T(1,128)} reshape(f32[32,16,3,3,3]{4,3,2,1,0:T(4,128)S(1)} %copy.23) | data formatting | bytes 110592 | tf_op jit(solution)/shard_map/reshape | solution.py:394
  61.1 12.2 %shard_map.69 = (f32[1,432]{1,0:T(1,128)}, f32[1,1728]{1,0:T(1,128)}) custom-call(f32[4,1,432]{2,1,0:T(1,128)} %reshape.83.g1_ref, f32[8,1,1728]{2,1,0:T(1,128)} %reshape.84.g2_ref), custom_call_target="tpu_custom_call" | custom-call | tf_op jit(solution)/shard_map/pallas_call | solution.py:396
  73.4 1.3 %reduce.2 = f32[1728]{0:T(1024)} reduce(f32[1,1728]{1,0:T(1,128)} %get-tuple-element.20, f32[]{:T(128)} %constant.18), dimensions={0}, to_apply=%get-tuple-element.20.reduce_sub_computation | reduce | bytes 13828 | tf_op jit(solution)/shard_map/pallas_call | solution.py:396
  74.7 1.2 %copy.38 = f32[432]{0:T(512)} copy(f32[432]{0:T(512)} %bitcast.45) | data formatting | bytes 3456
  (8 shorter events, 0.1 us)

commit v2 on v1

--- a/solution.py
+++ b/solution.py
@@ -153,14 +153,94 @@
     return lax.dot_general(a, b, (((1,), (1,)), ((), ())), preferred_element_type=F32)
 
 
+def one_hot(rows, source):
+    row = lax.broadcasted_iota(jnp.int32, (rows, source.shape[1]), 0)
+    return jnp.where(row == source, 1.0, 0.0).astype(BF16)
+
+
+def build_selectors(q1, q2, q3):
+    lane = lax.broadcasted_iota(jnp.int32, (1, 256), 1)
+    kx, ky, i = lane >> 6, (lane >> 2) & 15, lane & 3
+    source1 = jnp.where((kx < 3) & (ky < 3), i * 27 + kx * 9 + ky * 3, -9)
+    kx, ky, i = lane >> 6, (lane >> 4) & 3, lane & 15
+    source2 = jnp.where((kx < 3) & (ky < 3), i * 27 + kx * 9 + ky * 3, -9)
+    for kz in range(3):
+        q1[kz] = one_hot(27 * CIN, source1 + kz)
+        q2[kz] = one_hot(27 * C1, source2 + kz)
+    lane = lax.broadcasted_iota(jnp.int32, (1, 128), 1)
+    kz, i = lane >> 4, lane & 15
+    for kx in range(3):
+        for ky in range(3):
+            source3 = jnp.where(kz < 3, i * 27 + (2 - kx) * 9 + (2 - ky) * 3 + 2 - kz, -9)
+            q3[3 * kx + ky] = one_hot(27 * C1, source3)
+
+
+def gather_rows(all_ref, rows_ref, wide_ref):
+    owners, count, unit = all_ref.shape
+    for j in range(owners):
+        rows_ref[count * j : count * (j + 1)] = all_ref[j].astype(F32)
+    split = wide_ref.shape[1] // unit
+    if split == 1:
+        return rows_ref[...].astype(BF16)
+    for k in range(split):
+        wide_ref[:, unit * k : unit * (k + 1)] = rows_ref[pl.ds(k, wide_ref.shape[0], stride=split)]
+    return wide_ref[...].astype(BF16)
+
+
+def scatter_rows(value, rows_ref, wide_ref, out_ref):
+    owners, count, unit = out_ref.shape
+    split = value.shape[1] // unit
+    if split == 1:
+        rows_ref[...] = value
+    else:
+        wide_ref[...] = value
+        for k in range(split):
+            rows_ref[pl.ds(k, value.shape[0], stride=split)] = wide_ref[:, unit * k : unit * (k + 1)]
+    for j in range(owners):
+        out_ref[j] = rows_ref[count * j : count * (j + 1)]
+
+
+def flat_order(grad, q, chans):
+    result = 0.0
+    for kz in range(3):
+        g = grad[chans * kz : chans * (kz + 1)]
+        high = g.astype(BF16)
+        rest = g - high.astype(F32)
+        mid = rest.astype(BF16)
+        low = (rest - mid.astype(F32)).astype(BF16)
+        r = dot_nt(jnp.concatenate([high, mid, low], axis=0), q[kz])
+        result = result + (r[:chans] + r[chans : 2 * chans] + r[2 * chans :])
+    return result
+
+
 def compute_kernel(
-    n_space, n_samp, v_ref, c_ref, w1_ref, w2_ref, w3_ref, act_ref, o1_ref, o2_ref,
+    n_space, n_samp, vp_ref, c_ref, all1_ref, all2_ref, act_ref, o1_ref, o2_ref,
     a1, a2, a3, hid, back, pre, t1, perm, acc1, acc2, act,
+    q1, q2, q3, rows1, wide1, rows2, wide2, tall3, vf, v_ref,
 ):
     s = lax.axis_index("space")
     m = lax.axis_index("samp")
-    size_z = v_ref.shape[-1]
+    size_z = vp_ref.shape[-1]
     last = size_z - 1
+    build_selectors(q1, q2, q3)
+    m1 = gather_rows(all1_ref, rows1, wide1)
+    m2 = gather_rows(all2_ref, rows2, wide2)
+    base1 = jnp.concatenate([dot(m1, q1[kz]) for kz in range(3)], axis=0)
+    base2 = jnp.concatenate([dot(m2, q2[kz]) for kz in range(3)], axis=0)
+    tall3[...] = jnp.zeros_like(tall3)
+    for kx in range(3):
+        for ky in range(3):
+            start = 128 * kx + C2 * ky
+            tall3[start : start + C2] = dot(m2, q3[3 * kx + ky])
+    base3 = tall3[...].T[:48]
+
+    def lift(x, carry):
+        for y in range(vp_ref.shape[1]):
+            vf[CIN * y : CIN * (y + 1)] = vp_ref[x, y].astype(F32)
+        v_ref[x] = vf[...].astype(BF16)
+        return carry
+
+    lax.fori_loop(0, vp_ref.shape[0], lift, 0)
     size_x, size_y = act_ref.shape[1], act_ref.shape[2]
     high_y = size_y + 4
 
@@ -169,14 +249,11 @@
 
     lane1 = lanes(C1)
     lane2 = lanes(C2)
-    base1 = w1_ref[...]
     for y in range(high_y):
         row = base1 if y == 0 else pltpu.roll(base1, 4 * y, axis=1)
         a1[48 * y : 48 * y + 48] = row[:, :192].astype(BF16)
-    base2 = w2_ref[...]
     a2[:96] = base2[:, :192].astype(BF16)
     a2[96:] = pltpu.roll(base2, 16, axis=1)[:, :192].astype(BF16)
-    base3 = w3_ref[...]
     a3[:48] = base3.astype(BF16)
     a3[48:] = pltpu.roll(base3, 32, axis=1).astype(BF16)
     r = lax.broadcasted_iota(jnp.int32, (C2 * size_y, C2 * size_y), 0)
@@ -246,11 +323,12 @@
     def wide(values, rows):
         return jnp.concatenate([values, jnp.zeros((rows, 64), F32)], axis=1)
 
-    o2_ref[...] = wide(acc2[:96], 96) + pltpu.roll(wide(acc2[96:], 96), 256 - 16, axis=1)
+    total2 = wide(acc2[:96], 96) + pltpu.roll(wide(acc2[96:], 96), 256 - 16, axis=1)
     total = jnp.zeros((48, 256), F32)
     for y in range(size_y):
         total = total + pltpu.roll(wide(acc1[48 * y : 48 * y + 48], 48), 256 - 4 * (y + 2), axis=1)
-    o1_ref[...] = total
+    scatter_rows(flat_order(total, q1, C1), rows1, wide1, o1_ref)
+    scatter_rows(flat_order(total2, q2, C2), rows2, wide2, o2_ref)
 
 
 def reduce_kernel(
@@ -330,6 +408,10 @@
     _, size_x, size_y, size_z = volume.shape
     len1 = filters_one.shape[0]
     len2 = filters_two.shape[0]
+    unit1 = math.gcd(len1, 27 * CIN)
+    unit2 = math.gcd(len2, 27 * C1)
+    piece1 = (len1 // unit1, unit1)
+    piece2 = (len2 // unit2, unit2)
     sem = pltpu.SemaphoreType.DMA
     v_rows = volume.transpose(1, 2, 0, 3)
     c_rows = cotangent.transpose(1, 2, 0, 3)
@@ -338,8 +420,8 @@
         out_shape=[
             jax.ShapeDtypeStruct((size_x + 6, size_y + 8, CIN, size_z), BF16),
             jax.ShapeDtypeStruct((size_x + 2, size_y + 2, C2, size_z), BF16),
-            jax.ShapeDtypeStruct((n_samp, 1, len1), BF16),
-            jax.ShapeDtypeStruct((n_space, 1, len2), BF16),
+            jax.ShapeDtypeStruct((n_samp, *piece1), BF16),
+            jax.ShapeDtypeStruct((n_space, *piece2), BF16),
         ],
         in_specs=[VMEM] * 4,
         out_specs=[VMEM] * 4,
@@ -349,28 +431,17 @@
         ],
         compiler_params=pltpu.CompilerParams(
             collective_id=0, has_side_effects=True, vmem_limit_bytes=40 * 2**20),
-    )(v_rows, c_rows, filters_one.reshape(1, len1), filters_two.reshape(1, len2))
-
-    kern1 = all1.reshape(C1, CIN, 3, 3, 3).astype(F32)
-    kern2 = all2.reshape(C2, C1, 3, 3, 3).astype(F32)
-    base1 = kern1.transpose(4, 0, 2, 3, 1).reshape(3 * C1, 3, 3 * CIN)
-    base1 = jnp.pad(base1, ((0, 0), (0, 0), (0, 64 - 3 * CIN))).reshape(3 * C1, 192)
-    base1 = jnp.pad(base1, ((0, 0), (0, 64)))
-    base2 = kern2.transpose(4, 0, 2, 3, 1).reshape(3 * C2, 3, 3 * C1)
-    base2 = jnp.pad(base2, ((0, 0), (0, 0), (0, 64 - 3 * C1))).reshape(3 * C2, 192)
-    base2 = jnp.pad(base2, ((0, 0), (0, 64)))
-    base3 = jnp.flip(kern2, (2, 3, 4)).transpose(4, 1, 2, 3, 0).reshape(3 * C1, 3, 3 * C2)
-    base3 = jnp.pad(base3, ((0, 0), (0, 0), (0, 128 - 3 * C2))).reshape(3 * C1, 384)
+    )(v_rows, c_rows, filters_one.reshape(piece1), filters_two.reshape(piece2))
 
     high_y = size_y + 4
     activation, grad1, grad2 = pl.pallas_call(
         functools.partial(compute_kernel, n_space, n_samp),
         out_shape=[
             jax.ShapeDtypeStruct((C2, size_x, size_y, size_z), BF16),
-            jax.ShapeDtypeStruct((48, 256), F32),
-            jax.ShapeDtypeStruct((96, 256), F32),
+            jax.ShapeDtypeStruct((n_samp, *piece1), F32),
+            jax.ShapeDtypeStruct((n_space, *piece2), F32),
         ],
-        in_specs=[VMEM] * 5,
+        in_specs=[VMEM] * 4,
         out_specs=[VMEM] * 3,
         scratch_shapes=[
             pltpu.VMEM((48 * high_y, 192), BF16),
@@ -384,30 +455,36 @@
             pltpu.VMEM((48 * size_y, 192), F32),
             pltpu.VMEM((192, 192), F32),
             pltpu.VMEM((size_x + 2, C2 * (size_y + 2), size_z), BF16),
+            pltpu.VMEM((3, 27 * CIN, 256), BF16),
+            pltpu.VMEM((3, 27 * C1, 256), BF16),
+            pltpu.VMEM((9, 27 * C1, 128), BF16),
+            pltpu.VMEM((n_samp * piece1[0], piece1[1]), F32),
+            pltpu.VMEM((C1, 27 * CIN), F32),
+            pltpu.VMEM((n_space * piece2[0], piece2[1]), F32),
+            pltpu.VMEM((C2, 27 * C1), F32),
+            pltpu.VMEM((384, 128), F32),
+            pltpu.VMEM((CIN * (size_y + 8), size_z), F32),
+            pltpu.VMEM((size_x + 6, CIN * (size_y + 8), size_z), BF16),
         ],
         compiler_params=pltpu.CompilerParams(vmem_limit_bytes=48 * 2**20),
-    )(vp.reshape(size_x + 6, CIN * (size_y + 8), size_z), cp, base1, base2, base3)
-
-    grad1 = grad1[:, :192].reshape(3, C1, 3, 64)[..., : 3 * CIN].reshape(3, C1, 3, 3, CIN)
-    grad1 = grad1.transpose(1, 4, 2, 3, 0).reshape(n_samp, 1, len1)
-    grad2 = grad2[:, :192].reshape(3, C2, 3, 64)[..., : 3 * C1].reshape(3, C2, 3, 3, C1)
-    grad2 = grad2.transpose(1, 4, 2, 3, 0).reshape(n_space, 1, len2)
+    )(vp, cp, all1, all2)
+
     scale = 1.0 / math.sqrt(float(size_x * n_space * size_y * n_samp * size_z))
     out1, out2 = pl.pallas_call(
         functools.partial(reduce_kernel, n_space, n_samp, scale),
         out_shape=[
-            jax.ShapeDtypeStruct((1, len1), F32),
-            jax.ShapeDtypeStruct((1, len2), F32),
+            jax.ShapeDtypeStruct(piece1, F32),
+            jax.ShapeDtypeStruct(piece2, F32),
         ],
         in_specs=[VMEM] * 2,
         out_specs=[VMEM] * 2,
         scratch_shapes=[
-            pltpu.VMEM((n_samp, 1, len1), F32),
-            pltpu.VMEM((n_space, 1, len2), F32),
-            pltpu.VMEM((n_space, 1, len1), F32),
-            pltpu.VMEM((n_samp, 1, len2), F32),
-            pltpu.VMEM((1, len1), F32),
-            pltpu.VMEM((1, len2), F32),
+            pltpu.VMEM((n_samp, *piece1), F32),
+            pltpu.VMEM((n_space, *piece2), F32),
+            pltpu.VMEM((n_space, *piece1), F32),
+            pltpu.VMEM((n_samp, *piece2), F32),
+            pltpu.VMEM(piece1, F32),
+            pltpu.VMEM(piece2, F32),
             sem((n_samp,)), sem((n_samp,)), sem((n_space,)), sem((n_space,)),
             sem((n_space,)), sem((n_space,)), sem((n_samp,)), sem((n_samp,)),
         ],

time: 76.7 us -> 48 us (0.63)
  local copies, waits for them, and re-layouts: 35.2 us -> 7.67 us
  other arithmetic: 1.5 us -> 0 us
  Pallas kernels: 38.5 us -> 39.3 us
    rev x1 -> x0, local copies, waits for them, and re-layouts: 10.5 us -> none  [on_device(): jnp.flip(kern2, (2, 3, 4)).transpose(4, 1, 2, 3, 0)]
    transpose x4 -> x0, local copies, waits for them, and re-layouts: 7.61 us -> none  [the longest x1 3.54 us: on_device(): grad2 = grad2.transpose(1, 4, 2, 3, 0).reshape(n_space, 1, len2)]
    convert_element_type x2 -> x0, local copies, waits for them, and re-layouts: 3.75 us -> none  [the longest x1 3.49 us: on_device(): kern2 = all2.reshape(C2, C1, 3, 3, 3).astype(F32)]
    unnamed x6 -> x8, local copies, waits for them, and re-layouts: 7.29 us -> 4.1 us
    reshape x12 -> x4, local copies, waits for them, and re-layouts: 5.76 us -> 3.57 us  [the longest x2 2.03 us: on_device(): return (activation, out1.reshape(len1), out2.reshape(len2))]
    pallas_call x2 -> x0, other arithmetic: 1.35 us -> none  [the longest x1 1.31 us: on_device(): pl.pallas_call(functools.partial(reduce_kernel, n_space, n_samp, scale),...]
    pallas_call x1, Pallas kernels: 9.01 us -> 10.1 us  [on_device(): pl.pallas_call(functools.partial(compute_kernel, n_space, n_samp), out_sh...]
where the time goes in v2:
time: 48 us; the launch traced here: 47.6 us
  Pallas kernels  39.3 us (82%)
  local copies, waits for them, and re-layouts  7.67 us (16%)
  between operations  0.66 us (1%)
    pallas_call x1, Pallas kernels, on_device(): pl.pallas_call(functools.partial(exchange_kernel, n_space, n_samp), out_s...  16.9 us
    pallas_call x1, Pallas kernels, on_device(): pl.pallas_call(functools.partial(reduce_kernel, n_space, n_samp, scale),...  12.3 us
    pallas_call x1, Pallas kernels, on_device(): pl.pallas_call(functools.partial(compute_kernel, n_space, n_samp), out_sh...  10.1 us
    unnamed x8, local copies, waits for them, and re-layouts  4.1 us
    reshape x2, local copies, waits for them, and re-layouts, on_device(): return (activation, out1.reshape(len1), out2.reshape(len2))  2.03 us

profile of v2, /device:TPU:0, one launch (start us, length us, event | category | flops | bytes accessed | tf_op | source)
XLA Modules:
  0.0 47.6 jit_solution(17058132963217572802)
XLA Ops:
  0.6 0.8 %reshape.18.f1_ref = bf16[4,108]{1,0:T(4,128)(2,1)S(1)} reshape(bf16[432]{0:T(512)(128)(2,1)} %param.5) | data formatting | bytes 1728 | tf_op jit(solution)/shard_map/reshape | solution.py:434
  1.4 0.8 %reshape.19.f2_ref = bf16[4,432]{1,0:T(4,128)(2,1)S(1)} reshape(bf16[1728]{0:T(1024)(128)(2,1)} %param.6) | data formatting | bytes 6912 | tf_op jit(solution)/shard_map/reshape | solution.py:434
  2.2 0.9 %copy.12 = bf16[4,4,8,256]{3,0,2,1:T(4,128)(2,1)S(1)} copy(bf16[4,4,8,256]{3,2,1,0:T(8,128)(2,1)} %param.4) | data formatting | bytes 131072 | tf_op args[0]
  3.1 1.3 %copy.11 = bf16[32,4,8,256]{3,0,2,1:T(8,128)(2,1)S(1)} copy(bf16[32,4,8,256]{3,2,1,0:T(8,128)(2,1)} %param.7) | data formatting | bytes 1048576 | tf_op args[3]
  4.4 16.9 %shard_map.67 = (bf16[10,16,4,256]{3,2,1,0:T(4,128)(2,1)S(1)}, bf16[6,10,32,256]{3,2,1,0:T(8,128)(2,1)S(1)}, bf16[4,4,108]{2,1,0:T(4,128)(2,1)S(1)}, bf16[8,4,432]{2,1,0:T(4,128)(2,1)S(1)}) custom-call(bf16[4,8,4,256]{3,2,1,0:T(4,128)(2,1)S(1)} %bitcast.7, bf16[4,8,32,256]{3,2,1,0:T(8,128)(2,1)S(1)} %bitcast.6, bf16[4,108]{1,0:T(4,128)(2,1)S(1)} %reshape.18.f1_ref, ...), custom_call_target="tpu_custom_call" | custom-call | tf_op jit(solution)/shard_map/pallas_call | solution.py:418
  21.4 10.1 %shard_map.68 = (bf16[32,4,8,256]{3,2,1,0:T(8,128)(2,1)}, f32[4,4,108]{2,1,0:T(4,128)S(1)}, f32[8,4,432]{2,1,0:T(4,128)S(1)}) custom-call(bf16[10,16,4,256]{3,2,1,0:T(4,128)(2,1)S(1)} %get-tuple-element.12.vp_ref, bf16[6,10,32,256]{3,2,1,0:T(8,128)(2,1)S(1)} %get-tuple-element.13.c_ref, bf16[4,4,108]{2,1,0:T(4,128)(2,1)S(1)} %get-tuple-element.14.all1_ref, ...), custom_call_target="tpu_custom_call" | custom-call | tf_op jit(solution)/shard_map/pallas_call | solution.py:437
  31.5 0.0 copy-start
  31.5 0.6 %copy-done = f32[8,4,432]{2,1,0:T(4,128)} copy-done((f32[8,4,432]{2,1,0:T(4,128)}, f32[8,4,432]{2,1,0:T(4,128)S(1)}, u32[]{:S(2)}) %copy-start) | copy-done | bytes 55320
  32.1 0.0 copy-start.1
  32.1 0.6 %copy-done.1 = f32[4,4,108]{2,1,0:T(4,128)} copy-done((f32[4,4,108]{2,1,0:T(4,128)}, f32[4,4,108]{2,1,0:T(4,128)S(1)}, u32[]{:S(2)}) %copy-start.1) | copy-done | bytes 6936
  32.7 12.3 %shard_map.69 = (f32[4,108]{1,0:T(4,128)}, f32[4,432]{1,0:T(4,128)}) custom-call(f32[4,4,108]{2,1,0:T(4,128)} %copy-done.1, f32[8,4,432]{2,1,0:T(4,128)} %copy-done), custom_call_target="tpu_custom_call" | custom-call | tf_op jit(solution)/shard_map/pallas_call | solution.py:473
  44.9 0.0 copy-start.2
  45.0 0.7 %copy-done.2 = f32[4,108]{1,0:T(4,128)S(1)} copy-done((f32[4,108]{1,0:T(4,128)S(1)}, f32[4,108]{1,0:T(4,128)}, u32[]{:S(2)}) %copy-start.2) | copy-done | bytes 1752
  45.6 0.7 %reshape.20 = f32[432]{0:T(512)} reshape(f32[4,108]{1,0:T(4,128)S(1)} %copy-done.2) | data formatting | bytes 3456 | tf_op jit(solution)/shard_map/reshape | solution.py:493
  46.3 1.4 %reshape.21 = f32[1728]{0:T(1024)} reshape(f32[4,432]{1,0:T(4,128)} %get-tuple-element.20) | data formatting | bytes 13824 | tf_op jit(solution)/shard_map/reshape | solution.py:493
Async XLA Ops:
  31.5 0.6 %copy-start = (f32[8,4,432]{2,1,0:T(4,128)}, f32[8,4,432]{2,1,0:T(4,128)S(1)}, u32[]{:S(2)}) copy-start(f32[8,4,432]{2,1,0:T(4,128)S(1)} %get-tuple-element.18.g2_ref) | copy-start | bytes 165892
  32.1 0.6 %copy-start.1 = (f32[4,4,108]{2,1,0:T(4,128)}, f32[4,4,108]{2,1,0:T(4,128)S(1)}, u32[]{:S(2)}) copy-start(f32[4,4,108]{2,1,0:T(4,128)S(1)} %get-tuple-element.17.g1_ref) | copy-start | bytes 20740
  44.9 0.7 %copy-start.2 = (f32[4,108]{1,0:T(4,128)S(1)}, f32[4,108]{1,0:T(4,128)}, u32[]{:S(2)}) copy-start(f32[4,108]{1,0:T(4,128)} %get-tuple-element.19) | copy-start | bytes 5188

commit v3 on v2

v3 whole, which is shorter than its diff:
```python
import functools
import math

import jax
import jax.numpy as jnp
from jax import lax
from jax.experimental import pallas as pl
from jax.experimental.pallas import tpu as pltpu
from jax.sharding import PartitionSpec as P

CIN = 4
C1 = 16
C2 = 32
SLOPE = 0.3
MESH = pl.DeviceIdType.MESH
F32 = jnp.float32
BF16 = jnp.bfloat16
DIRS = [(dx, dy) for dx in (-1, 0, 1) for dy in (-1, 0, 1) if (dx, dy) != (0, 0)]


def spans(delta, size, width):
    if delta == 1:
        return (size - width, width), (0, width)
    if delta == -1:
        return (0, width), (size + width, width)
    return (0, size), (width, size)


def leaky(values):
    return jnp.where(values > 0, values, SLOPE * values)


def tap_sum(t, rows, lane, last):
    low = jnp.where(lane == 0, 0.0, pltpu.roll(t[:rows], 1, axis=1))
    high = jnp.where(lane == last, 0.0, pltpu.roll(t[2 * rows :], last, axis=1))
    return t[rows : 2 * rows] + low + high


def tap_spread(b, lane, last):
    low = jnp.where(lane == last, 0.0, pltpu.roll(b, last, axis=1))
    high = jnp.where(lane == 0, 0.0, pltpu.roll(b, 1, axis=1))
    return jnp.concatenate([low, b, high], axis=0)


def dot(a, b):
    return lax.dot_general(a, b, (((1,), (0,)), ((), ())), preferred_element_type=F32)


def dot_nt(a, b):
    return lax.dot_general(a, b, (((1,), (1,)), ((), ())), preferred_element_type=F32)


def one_hot(rows, source):
    row = lax.broadcasted_iota(jnp.int32, (rows, source.shape[1]), 0)
    return jnp.where(row == source, 1.0, 0.0).astype(BF16)


def build_selectors(q1, q2, q3):
    lane = lax.broadcasted_iota(jnp.int32, (1, 256), 1)
    kx, ky, i = lane >> 6, (lane >> 2) & 15, lane & 3
    source1 = jnp.where((kx < 3) & (ky < 3), i * 27 + kx * 9 + ky * 3, -9)
    kx, ky, i = lane >> 6, (lane >> 4) & 3, lane & 15
    source2 = jnp.where((kx < 3) & (ky < 3), i * 27 + kx * 9 + ky * 3, -9)
    for kz in range(3):
        q1[kz] = one_hot(27 * CIN, source1 + kz)
        q2[kz] = one_hot(27 * C1, source2 + kz)
    lane = lax.broadcasted_iota(jnp.int32, (1, 128), 1)
    kz, i = lane >> 4, lane & 15
    for kx in range(3):
        for ky in range(3):
            source3 = jnp.where(kz < 3, i * 27 + (2 - kx) * 9 + (2 - ky) * 3 + 2 - kz, -9)
            q3[3 * kx + ky] = one_hot(27 * C1, source3)


def gather_rows(all_ref, rows_ref, wide_ref):
    owners, count, unit = all_ref.shape
    for j in range(owners):
        rows_ref[count * j : count * (j + 1)] = all_ref[j].astype(F32)
    split = wide_ref.shape[1] // unit
    if split == 1:
        return rows_ref[...].astype(BF16)
    for k in range(split):
        wide_ref[:, unit * k : unit * (k + 1)] = rows_ref[pl.ds(k, wide_ref.shape[0], stride=split)]
    return wide_ref[...].astype(BF16)


def scatter_rows(value, rows_ref, wide_ref, out_ref):
    owners, count, unit = out_ref.shape
    split = value.shape[1] // unit
    if split == 1:
        rows_ref[...] = value
    else:
        wide_ref[...] = value
        for k in range(split):
            rows_ref[pl.ds(k, value.shape[0], stride=split)] = wide_ref[:, unit * k : unit * (k + 1)]
    for j in range(owners):
        out_ref[j] = rows_ref[count * j : count * (j + 1)]


def flat_order(grad, q, chans):
    result = 0.0
    for kz in range(3):
        g = grad[chans * kz : chans * (kz + 1)]
        high = g.astype(BF16)
        rest = g - high.astype(F32)
        mid = rest.astype(BF16)
        low = (rest - mid.astype(F32)).astype(BF16)
        r = dot_nt(jnp.concatenate([high, mid, low], axis=0), q[kz])
        result = result + (r[:chans] + r[chans : 2 * chans] + r[2 * chans :])
    return result


def fused_kernel(
    n_space, n_samp, scale, v_ref, c_ref, f1_ref, f2_ref, act_ref, o1_ref, o2_ref,
    vp, cp, all1, all2,
    a1, a2, a3, hid, back, pre, t1, perm, acc1, acc2, act,
    q1, q2, q3, rows1, wide1, rows2, wide2, tall3, vf, vrows,
    grad1, grad2, part1, part2, full1, full2, mine1, mine2,
    send_v, recv_v, send_c, recv_c, send_1, recv_1, send_2, recv_2,
    send_a1, recv_a1, send_a2, recv_a2, send_b1, recv_b1, send_b2, recv_b2,
):
    s = lax.axis_index("space")
    m = lax.axis_index("samp")
    size_x, size_y = v_ref.shape[0], v_ref.shape[1]

    vp[...] = jnp.zeros_like(vp)

    def zero_row(x, carry):
        cp[x] = jnp.zeros(cp.shape[1:], cp.dtype)
        return carry

    lax.fori_loop(0, cp.shape[0], zero_row, 0)

    def there(dx, dy):
        return (s + dx >= 0) & (s + dx < n_space) & (m + dy >= 0) & (m + dy < n_samp)

    barrier = pltpu.get_barrier_semaphore()
    peers = n_samp - 1 + n_space - 1
    for dx, dy in DIRS:
        if dx == 0 or dy == 0:
            continue
        peers = peers + jnp.where(there(dx, dy), 1, 0)

        @pl.when(there(dx, dy))
        def _():
            pl.semaphore_signal(barrier, inc=1, device_id=(s + dx, m + dy), device_id_type=MESH)
    for k in range(1, n_samp):
        pl.semaphore_signal(barrier, inc=1, device_id=(s, lax.rem(m + k, n_samp)), device_id_type=MESH)

    def greet(k, carry):
        pl.semaphore_signal(barrier, inc=1, device_id=(lax.rem(s + k, n_space), m), device_id_type=MESH)
        return carry

    lax.fori_loop(1, n_space, greet, 0)
    pl.semaphore_wait(barrier, peers)

    def copy_1(k):
        return pltpu.make_async_remote_copy(
            src_ref=f1_ref, dst_ref=all1.at[m], send_sem=send_1.at[k], recv_sem=recv_1.at[k],
            device_id=(s, lax.rem(m + k, n_samp)), device_id_type=MESH)

    def copy_2(k):
        return pltpu.make_async_remote_copy(
            src_ref=f2_ref, dst_ref=all2.at[s], send_sem=send_2.at[k], recv_sem=recv_2.at[k],
            device_id=(lax.rem(s + k, n_space), m), device_id_type=MESH)

    def halo(src, dst, width, send, recv, slot, dx, dy):
        (sx, nx), (tx, _) = spans(dx, size_x, width)
        (sy, ny), (ty, _) = spans(dy, size_y, width)
        return pltpu.make_async_remote_copy(
            src_ref=src.at[pl.ds(sx, nx), pl.ds(sy, ny)], dst_ref=dst.at[pl.ds(tx, nx), pl.ds(ty, ny)],
            send_sem=send.at[slot], recv_sem=recv.at[slot],
            device_id=(jnp.clip(s + dx, 0, n_space - 1), jnp.clip(m + dy, 0, n_samp - 1)),
            device_id_type=MESH)

    vol = [halo(v_ref, vp, 3, send_v, recv_v, j, dx, dy) for j, (dx, dy) in enumerate(DIRS)]
    cot = [halo(c_ref, cp, 1, send_c, recv_c, j, dx, dy) for j, (dx, dy) in enumerate(DIRS)]
    for k in range(1, n_samp):
        copy_1(k).start()

    def start_2(k, carry):
        copy_2(k).start()
        return carry

    lax.fori_loop(1, n_space, start_2, 0)
    for group in (vol, cot):
        for copy, (dx, dy) in zip(group, DIRS):
            @pl.when(there(dx, dy))
            def _():
                copy.start()

    all1[m] = f1_ref[...]
    all2[s] = f2_ref[...]
    vp[3 : 3 + size_x, 3 : 3 + size_y] = v_ref[...]

    def centre(x, carry):
        cp[x + 1, 1 : 1 + size_y] = c_ref[x]
        return carry

    lax.fori_loop(0, size_x, centre, 0)


    size_z = v_ref.shape[-1]
    last = size_z - 1
    high_y = size_y + 4

    def lanes(rows):
        return lax.broadcasted_iota(jnp.int32, (rows, size_z), 1)

    lane1 = lanes(C1)
    lane2 = lanes(C2)
    build_selectors(q1, q2, q3)
    r = lax.broadcasted_iota(jnp.int32, (C2 * size_y, C2 * size_y), 0)
    q = lax.broadcasted_iota(jnp.int32, (C2 * size_y, C2 * size_y), 1)
    from_row = (r % size_y) * C2 + r // size_y
    perm[...] = jnp.where(q == from_row, 1.0, 0.0).astype(BF16)
    acc1[...] = jnp.zeros_like(acc1)
    acc2[...] = jnp.zeros_like(acc2)
    tall3[...] = jnp.zeros_like(tall3)

    def over_space(body):
        def step(k, carry):
            body(k)
            return carry

        lax.fori_loop(1, n_space, step, 0)

    def arrive(group):
        for copy, (dx, dy) in zip(group, DIRS):
            @pl.when(there(-dx, -dy))
            def _():
                copy.wait_recv()

            @pl.when(there(dx, dy))
            def _():
                copy.wait_send()

    for k in range(1, n_samp):
        copy_1(k).wait()
    over_space(lambda k: copy_2(k).wait())
    m1 = gather_rows(all1, rows1, wide1)
    m2 = gather_rows(all2, rows2, wide2)
    base1 = jnp.concatenate([dot(m1, q1[kz]) for kz in range(3)], axis=0)
    base2 = jnp.concatenate([dot(m2, q2[kz]) for kz in range(3)], axis=0)
    for kx in range(3):
        for ky in range(3):
            first = 128 * kx + C2 * ky
            tall3[first : first + C2] = dot(m2, q3[3 * kx + ky])
    base3 = tall3[...].T[:48]
    for y in range(high_y):
        row = base1 if y == 0 else pltpu.roll(base1, 4 * y, axis=1)
        a1[48 * y : 48 * y + 48] = row[:, :192].astype(BF16)
    a2[:96] = base2[:, :192].astype(BF16)
    a2[96:] = pltpu.roll(base2, 16, axis=1)[:, :192].astype(BF16)
    a3[:48] = base3.astype(BF16)
    a3[48:] = pltpu.roll(base3, 32, axis=1).astype(BF16)

    arrive(vol)

    def lift(x, carry):
        for y in range(vp.shape[1]):
            vf[CIN * y : CIN * (y + 1)] = vp[x, y].astype(F32)
        vrows[x] = vf[...].astype(BF16)
        return carry

    lax.fori_loop(0, vp.shape[0], lift, 0)

    def vwin(x):
        return jnp.concatenate([vrows[x], vrows[x + 1], vrows[x + 2]], axis=0)

    def layer1(x, carry):
        gx = s * size_x + x - 2
        ok_x = (gx >= 0) & (gx < n_space * size_x)
        t1[...] = dot(a1[...], vwin(x))
        for y in range(high_y):
            gy = m * size_y + y - 2
            ok = ok_x & (gy >= 0) & (gy < n_samp * size_y)
            p = tap_sum(t1[48 * y : 48 * y + 48], C1, lane1, last)
            pre[x, 16 * y : 16 * y + 16] = p
            h = leaky(p) * jnp.where(ok, 1.0, 0.0)
            hid[x, 16 * y : 16 * y + 16] = h.astype(BF16)
        return carry

    lax.fori_loop(0, size_x + 4, layer1, 0)

    def hwin(x, y):
        return jnp.concatenate([hid[x + k, 16 * y : 16 * y + 64] for k in range(3)], axis=0)

    def pre_two(t, half):
        return tap_sum(t[96 * half : 96 * half + 96], C2, lane2, last)

    def back_two(x, y, p):
        b = (cp[x, y].astype(F32) * jnp.where(p > 0, 1.0, SLOPE)).astype(BF16)
        back[x, C2 * y : C2 * (y + 1)] = b
        return b

    def layer2(x, carry):
        moved, windows = [], []
        for y in range(1, 1 + size_y, 2):
            win = hwin(x + 1, y)
            t = dot(a2[...], win)
            both = []
            for half in range(2):
                p = pre_two(t, half)
                act[C2 * (y + half - 1) : C2 * (y + half)] = leaky(p).astype(BF16)
                b = back_two(x + 1, y + half, p)
                both.append(tap_spread(b.astype(F32), lane2, last).astype(BF16))
            moved.append(jnp.concatenate(both, axis=0))
            windows.append(win)
        acc2[...] += dot_nt(jnp.concatenate(moved, axis=1), jnp.concatenate(windows, axis=1))
        value = dot(perm[...], act[...])
        act_ref[:, x] = value.reshape(C2, size_y, size_z).astype(BF16)
        return carry

    lax.fori_loop(0, size_x, layer2, 0)

    def wide(values, rows):
        return jnp.concatenate([values, jnp.zeros((rows, 64), F32)], axis=1)

    def samp_peer(k):
        return lax.rem(m + k, n_samp)

    def space_peer(k):
        return lax.rem(s + k, n_space)

    def first_1(k):
        return pltpu.make_async_remote_copy(
            src_ref=grad1.at[samp_peer(k)], dst_ref=part1.at[m], send_sem=send_a1.at[k],
            recv_sem=recv_a1.at[k], device_id=(s, samp_peer(k)), device_id_type=MESH)

    def first_2(k):
        return pltpu.make_async_remote_copy(
            src_ref=grad2.at[space_peer(k)], dst_ref=part2.at[s], send_sem=send_a2.at[k],
            recv_sem=recv_a2.at[k], device_id=(space_peer(k), m), device_id_type=MESH)

    def second_1(k):
        return pltpu.make_async_remote_copy(
            src_ref=mine1, dst_ref=full1.at[s], send_sem=send_b1.at[k],
            recv_sem=recv_b1.at[k], device_id=(space_peer(k), m), device_id_type=MESH)

    def second_2(k):
        return pltpu.make_async_remote_copy(
            src_ref=mine2, dst_ref=full2.at[m], send_sem=send_b2.at[k],
            recv_sem=recv_b2.at[k], device_id=(s, samp_peer(k)), device_id_type=MESH)

    total2 = wide(acc2[:96], 96) + pltpu.roll(wide(acc2[96:], 96), 256 - 16, axis=1)
    scatter_rows(flat_order(total2, q2, C2), rows2, wide2, grad2)
    over_space(lambda k: first_2(k).start())
    part2[s] = grad2[s]

    arrive(cot)

    def edge_x(i, carry):
        x = (size_x + 1) * i
        for y in range(0, size_y + 2, 2):
            t = dot(a2[...], hwin(x, y))
            for half in range(2):
                back_two(x, y + half, pre_two(t, half))
        return carry

    lax.fori_loop(0, 2, edge_x, 0)

    def edge_y(x, carry):
        for half, y in ((0, 0), (1, size_y)):
            back_two(x + 1, y + half, pre_two(dot(a2[...], hwin(x + 1, y)), half))
        return carry

    lax.fori_loop(0, size_x, edge_y, 0)

    def finish(x, carry):
        pieces = []
        for y in range(0, size_y, 2):
            win = jnp.concatenate([back[x + k, C2 * y : C2 * y + 128] for k in range(3)], axis=0)
            t = dot(a3[...], win)
            for half in range(2):
                d = tap_sum(t[48 * half : 48 * half + 48], C1, lane1, last)
                p = pre[x + 2, 16 * (y + half + 2) : 16 * (y + half + 2) + 16]
                b1 = (d * jnp.where(p > 0, 1.0, SLOPE)).astype(BF16).astype(F32)
                pieces.append(tap_spread(b1, lane1, last).astype(BF16))
        acc1[...] += dot_nt(jnp.concatenate(pieces, axis=0), vwin(x + 2))
        return carry

    lax.fori_loop(0, size_x, finish, 0)

    total1 = jnp.zeros((48, 256), F32)
    for y in range(size_y):
        total1 = total1 + pltpu.roll(wide(acc1[48 * y : 48 * y + 48], 48), 256 - 4 * (y + 2), axis=1)
    scatter_rows(flat_order(total1, q1, C1), rows1, wide1, grad1)
    for k in range(1, n_samp):
        first_1(k).start()
    part1[m] = grad1[m]
    over_space(lambda k: first_2(k).wait())
    mine2[...] = jnp.sum(part2[...], axis=0)
    for k in range(1, n_samp):
        second_2(k).start()
    full2[m] = mine2[...]
    for k in range(1, n_samp):
        first_1(k).wait()
    mine1[...] = jnp.sum(part1[...], axis=0)
    over_space(lambda k: second_1(k).start())
    full1[s] = mine1[...]
    for k in range(1, n_samp):
        second_2(k).wait()
    o2_ref[...] = jnp.sum(full2[...], axis=0) * scale
    over_space(lambda k: second_1(k).wait())
    o1_ref[...] = jnp.sum(full1[...], axis=0) * scale


VMEM = pl.BlockSpec(memory_space=pltpu.VMEM)


def on_device(n_space, n_samp, volume, filters_one, filters_two, cotangent):
    _, size_x, size_y, size_z = volume.shape
    len1 = filters_one.shape[0]
    len2 = filters_two.shape[0]
    unit1 = math.gcd(len1, 27 * CIN)
    unit2 = math.gcd(len2, 27 * C1)
    piece1 = (len1 // unit1, unit1)
    piece2 = (len2 // unit2, unit2)
    high_y = size_y + 4
    scale = 1.0 / math.sqrt(float(size_x * n_space * size_y * n_samp * size_z))
    samp, space = pltpu.SemaphoreType.DMA((n_samp,)), pltpu.SemaphoreType.DMA((n_space,))
    sides = pltpu.SemaphoreType.DMA((8,))
    activation, out1, out2 = pl.pallas_call(
        functools.partial(fused_kernel, n_space, n_samp, scale),
        out_shape=[
            jax.ShapeDtypeStruct((C2, size_x, size_y, size_z), BF16),
            jax.ShapeDtypeStruct(piece1, F32),
            jax.ShapeDtypeStruct(piece2, F32),
        ],
        in_specs=[VMEM] * 4,
        out_specs=[VMEM] * 3,
        scratch_shapes=[
            pltpu.VMEM((size_x + 6, size_y + 8, CIN, size_z), BF16),
            pltpu.VMEM((size_x + 2, size_y + 2, C2, size_z), BF16),
            pltpu.VMEM((n_samp, *piece1), BF16),
            pltpu.VMEM((n_space, *piece2), BF16),
            pltpu.VMEM((48 * high_y, 192), BF16),
            pltpu.VMEM((192, 192), BF16),
            pltpu.VMEM((96, 384), BF16),
            pltpu.VMEM((size_x + 4, 16 * high_y, size_z), BF16),
            pltpu.VMEM((size_x + 2, C2 * (size_y + 2), size_z), BF16),
            pltpu.VMEM((size_x + 4, 16 * high_y, size_z), F32),
            pltpu.VMEM((48 * high_y, size_z), F32),
            pltpu.VMEM((C2 * size_y, C2 * size_y), BF16),
            pltpu.VMEM((48 * size_y, 192), F32),
            pltpu.VMEM((192, 192), F32),
            pltpu.VMEM((C2 * size_y, size_z), BF16),
            pltpu.VMEM((3, 27 * CIN, 256), BF16),
            pltpu.VMEM((3, 27 * C1, 256), BF16),
            pltpu.VMEM((9, 27 * C1, 128), BF16),
            pltpu.VMEM((n_samp * piece1[0], piece1[1]), F32),
            pltpu.VMEM((C1, 27 * CIN), F32),
            pltpu.VMEM((n_space * piece2[0], piece2[1]), F32),
            pltpu.VMEM((C2, 27 * C1), F32),
            pltpu.VMEM((384, 128), F32),
            pltpu.VMEM((CIN * (size_y + 8), size_z), F32),
            pltpu.VMEM((size_x + 6, CIN * (size_y + 8), size_z), BF16),
            pltpu.VMEM((n_samp, *piece1), F32),
            pltpu.VMEM((n_space, *piece2), F32),
            pltpu.VMEM((n_samp, *piece1), F32),
            pltpu.VMEM((n_space, *piece2), F32),
            pltpu.VMEM((n_space, *piece1), F32),
            pltpu.VMEM((n_samp, *piece2), F32),
            pltpu.VMEM(piece1, F32),
            pltpu.VMEM(piece2, F32),
            sides, sides, sides, sides, samp, samp, space, space,
            samp, samp, space, space, space, space, samp, samp,
        ],
        compiler_params=pltpu.CompilerParams(
            collective_id=0, has_side_effects=True, vmem_limit_bytes=48 * 2**20),
    )(volume.transpose(1, 2, 0, 3), cotangent.transpose(1, 2, 0, 3),
      filters_one.reshape(piece1), filters_two.reshape(piece2))
    return activation, out1.reshape(len1), out2.reshape(len2)


def solution(mesh):
    in_specs = (
        P(None, "space", "samp", None),
        P("samp"),
        P("space"),
        P(None, "space", "samp", None),
    )
    out_specs = (P(None, "space", "samp", None), P("samp"), P("space"))
    return jax.shard_map(
        functools.partial(on_device, mesh.shape["space"], mesh.shape["samp"]),
        mesh=mesh, in_specs=in_specs, out_specs=out_specs, check_vma=False,
    )
```

time: 48 us -> 39.3 us (0.82)
  Pallas kernels: 39.3 us -> 32.5 us
  local copies, waits for them, and re-layouts: 7.67 us -> 5.9 us
    pallas_call x3 -> x1, Pallas kernels: 39.3 us -> 32.5 us  [on_device(): pl.pallas_call(functools.partial(fused_kernel, n_space, n_samp, scale), o...]
    unnamed x8 -> x3, local copies, waits for them, and re-layouts: 4.1 us -> 3.02 us
    reshape x2, local copies, waits for them, and re-layouts: 2.03 us -> 1.34 us  [on_device(): return (activation, out1.reshape(len1), out2.reshape(len2))]
where the time goes in v3:
time: 39.3 us; the launch traced here: 39.1 us
  Pallas kernels  32.5 us (83%)
  local copies, waits for them, and re-layouts  5.9 us (15%)
  between operations  0.64 us (2%)
    pallas_call x1, Pallas kernels, on_device(): pl.pallas_call(functools.partial(fused_kernel, n_space, n_samp, scale), o...  32.5 us
    unnamed x3, local copies, waits for them, and re-layouts  3.02 us
    reshape x2, local copies, waits for them, and re-layouts, on_device(): return (activation, out1.reshape(len1), out2.reshape(len2))  1.34 us

profile of v3, /device:TPU:0, one launch (start us, length us, event | category | flops | bytes accessed | tf_op | source)
XLA Modules:
  0.0 39.1 jit_solution(8031719146321128338)
XLA Ops:
  0.6 0.8 %reshape.18.f1_ref = bf16[4,108]{1,0:T(4,128)(2,1)S(1)} reshape(bf16[432]{0:T(512)(128)(2,1)} %param.5) | data formatting | bytes 1728 | tf_op jit(solution)/shard_map/reshape | solution.py:473
  1.4 0.8 %reshape.19.f2_ref = bf16[4,432]{1,0:T(4,128)(2,1)S(1)} reshape(bf16[1728]{0:T(1024)(128)(2,1)} %param.6) | data formatting | bytes 6912 | tf_op jit(solution)/shard_map/reshape | solution.py:473
  2.2 0.9 %copy.12 = bf16[4,4,8,256]{3,0,2,1:T(4,128)(2,1)S(1)} copy(bf16[4,4,8,256]{3,2,1,0:T(8,128)(2,1)} %param.4) | data formatting | bytes 131072 | tf_op args[0]
  3.1 1.3 %copy.11 = bf16[32,4,8,256]{3,0,2,1:T(8,128)(2,1)S(1)} copy(bf16[32,4,8,256]{3,2,1,0:T(8,128)(2,1)} %param.7) | data formatting | bytes 1048576 | tf_op args[3]
  4.4 32.5 %shard_map.67 = (bf16[32,4,8,256]{3,2,1,0:T(8,128)(2,1)S(1)}, f32[4,108]{1,0:T(4,128)S(1)}, f32[4,432]{1,0:T(4,128)S(1)}) custom-call(bf16[4,8,4,256]{3,2,1,0:T(4,128)(2,1)S(1)} %bitcast.7, bf16[4,8,32,256]{3,2,1,0:T(8,128)(2,1)S(1)} %bitcast.6, bf16[4,108]{1,0:T(4,128)(2,1)S(1)} %reshape.18.f1_ref, bf16[4,432]{1,0:T(4,128)(2,1)S(1)} %reshape.19.f2_ref), custom_call_target="tpu_custom_call" | custom-call | tf_op jit(solution)/shard_map/pallas_call | solution.py:424
  37.0 0.7 %reshape.20 = f32[432]{0:T(512)} reshape(f32[4,108]{1,0:T(4,128)S(1)} %get-tuple-element.7) | data formatting | bytes 3456 | tf_op jit(solution)/shard_map/reshape | solution.py:474
  37.6 0.7 %reshape.21 = f32[1728]{0:T(1024)} reshape(f32[4,432]{1,0:T(4,128)S(1)} %get-tuple-element.8) | data formatting | bytes 13824 | tf_op jit(solution)/shard_map/reshape | solution.py:474
  38.3 0.8 %copy.14 = bf16[32,4,8,256]{3,2,1,0:T(8,128)(2,1)} copy(bf16[32,4,8,256]{3,2,1,0:T(8,128)(2,1)S(1)} %get-tuple-element.12) | data formatting | bytes 1048576

commit v4 on v3

--- a/solution.py
+++ b/solution.py
@@ -53,6 +53,12 @@
 def one_hot(rows, source):
     row = lax.broadcasted_iota(jnp.int32, (rows, source.shape[1]), 0)
     return jnp.where(row == source, 1.0, 0.0).astype(BF16)
+
+
+def one_hot_rows(chans, size_y):
+    r = lax.broadcasted_iota(jnp.int32, (chans * size_y, chans * size_y), 0)
+    q = lax.broadcasted_iota(jnp.int32, (chans * size_y, chans * size_y), 1)
+    return jnp.where(q == (r % chans) * size_y + r // chans, 1.0, 0.0).astype(BF16)
 
 
 def build_selectors(q1, q2, q3):
@@ -113,7 +119,7 @@
 def fused_kernel(
     n_space, n_samp, scale, v_ref, c_ref, f1_ref, f2_ref, act_ref, o1_ref, o2_ref,
     vp, cp, all1, all2,
-    a1, a2, a3, hid, back, pre, t1, perm, acc1, acc2, act,
+    turn, a1, a2, a3, hid, back, pre, t1, perm, acc1, acc2, act,
     q1, q2, q3, rows1, wide1, rows2, wide2, tall3, vf, vrows,
     grad1, grad2, part1, part2, full1, full2, mine1, mine2,
     send_v, recv_v, send_c, recv_c, send_1, recv_1, send_2, recv_2,
@@ -121,7 +127,7 @@
 ):
     s = lax.axis_index("space")
     m = lax.axis_index("samp")
-    size_x, size_y = v_ref.shape[0], v_ref.shape[1]
+    size_x, size_y, size_z = v_ref.shape[1:]
 
     vp[...] = jnp.zeros_like(vp)
 
@@ -152,6 +158,20 @@
         return carry
 
     lax.fori_loop(1, n_space, greet, 0)
+
+    turn[...] = one_hot_rows(C2, size_y)
+    turn_v = one_hot_rows(CIN, size_y)
+
+    def centre(x, carry):
+        value = c_ref[:, x].astype(F32).reshape(C2 * size_y, size_z).astype(BF16)
+        cp[x + 1, 1 : 1 + size_y] = dot(turn[...], value).astype(BF16).reshape(size_y, C2, size_z)
+        value = v_ref[:, x].astype(F32).reshape(CIN * size_y, size_z).astype(BF16)
+        value = dot(turn_v, value)
+        for y in range(size_y):
+            vp[x + 3, y + 3] = value[CIN * y : CIN * (y + 1)].astype(BF16)
+        return carry
+
+    lax.fori_loop(0, size_x, centre, 0)
     pl.semaphore_wait(barrier, peers)
 
     def copy_1(k):
@@ -168,13 +188,13 @@
         (sx, nx), (tx, _) = spans(dx, size_x, width)
         (sy, ny), (ty, _) = spans(dy, size_y, width)
         return pltpu.make_async_remote_copy(
-            src_ref=src.at[pl.ds(sx, nx), pl.ds(sy, ny)], dst_ref=dst.at[pl.ds(tx, nx), pl.ds(ty, ny)],
+            src_ref=src.at[pl.ds(sx + width, nx), pl.ds(sy + width, ny)], dst_ref=dst.at[pl.ds(tx, nx), pl.ds(ty, ny)],
             send_sem=send.at[slot], recv_sem=recv.at[slot],
             device_id=(jnp.clip(s + dx, 0, n_space - 1), jnp.clip(m + dy, 0, n_samp - 1)),
             device_id_type=MESH)
 
-    vol = [halo(v_ref, vp, 3, send_v, recv_v, j, dx, dy) for j, (dx, dy) in enumerate(DIRS)]
-    cot = [halo(c_ref, cp, 1, send_c, recv_c, j, dx, dy) for j, (dx, dy) in enumerate(DIRS)]
+    vol = [halo(vp, vp, 3, send_v, recv_v, j, dx, dy) for j, (dx, dy) in enumerate(DIRS)]
+    cot = [halo(cp, cp, 1, send_c, recv_c, j, dx, dy) for j, (dx, dy) in enumerate(DIRS)]
     for k in range(1, n_samp):
         copy_1(k).start()
 
@@ -191,16 +211,6 @@
 
     all1[m] = f1_ref[...]
     all2[s] = f2_ref[...]
-    vp[3 : 3 + size_x, 3 : 3 + size_y] = v_ref[...]
-
-    def centre(x, carry):
-        cp[x + 1, 1 : 1 + size_y] = c_ref[x]
-        return carry
-
-    lax.fori_loop(0, size_x, centre, 0)
-
-
-    size_z = v_ref.shape[-1]
     last = size_z - 1
     high_y = size_y + 4
 
@@ -435,6 +445,7 @@
             pltpu.VMEM((size_x + 2, size_y + 2, C2, size_z), BF16),
             pltpu.VMEM((n_samp, *piece1), BF16),
             pltpu.VMEM((n_space, *piece2), BF16),
+            pltpu.VMEM((C2 * size_y, C2 * size_y), BF16),
             pltpu.VMEM((48 * high_y, 192), BF16),
             pltpu.VMEM((192, 192), BF16),
             pltpu.VMEM((96, 384), BF16),
@@ -469,7 +480,7 @@
         ],
         compiler_params=pltpu.CompilerParams(
             collective_id=0, has_side_effects=True, vmem_limit_bytes=48 * 2**20),
-    )(volume.transpose(1, 2, 0, 3), cotangent.transpose(1, 2, 0, 3),
+    )(volume, cotangent,
       filters_one.reshape(piece1), filters_two.reshape(piece2))
     return activation, out1.reshape(len1), out2.reshape(len2)
 

time: 39.3 us -> 39 us (level)
    unnamed x3 -> x5, local copies, waits for them, and re-layouts: 3.02 us -> 2.68 us
where the time goes in v4:
time: 39 us; the launch traced here: 38.8 us
  Pallas kernels  32.6 us (84%)
  local copies, waits for them, and re-layouts  5.55 us (14%)
  between operations  0.64 us (2%)
    pallas_call x1, Pallas kernels, on_device(): pl.pallas_call(functools.partial(fused_kernel, n_space, n_samp, scale), o...  32.6 us
    unnamed x5, local copies, waits for them, and re-layouts  2.68 us
    reshape x2, local copies, waits for them, and re-layouts, on_device(): return (activation, out1.reshape(len1), out2.reshape(len2))  1.34 us

profile of v4, /device:TPU:0, one launch (start us, length us, event | category | flops | bytes accessed | tf_op | source)
XLA Modules:
  0.0 38.8 jit_solution(13823242158169358074)
XLA Ops:
  0.6 0.8 %reshape.18.f1_ref = bf16[4,108]{1,0:T(4,128)(2,1)S(1)} reshape(bf16[432]{0:T(512)(128)(2,1)} %param.5) | data formatting | bytes 1728 | tf_op jit(solution)/shard_map/reshape | solution.py:484
  1.4 0.8 %reshape.19.f2_ref = bf16[4,432]{1,0:T(4,128)(2,1)S(1)} reshape(bf16[1728]{0:T(1024)(128)(2,1)} %param.6) | data formatting | bytes 6912 | tf_op jit(solution)/shard_map/reshape | solution.py:484
  2.2 0.0 copy-start
  2.2 1.0 %copy-done = bf16[32,4,8,256]{3,2,1,0:T(8,128)(2,1)S(1)} copy-done((bf16[32,4,8,256]{3,2,1,0:T(8,128)(2,1)S(1)}, bf16[32,4,8,256]{3,2,1,0:T(8,128)(2,1)}, u32[]{:S(2)}) %copy-start) | copy-done | bytes 524312
  3.2 0.0 copy-start.1
  3.2 0.8 %copy-done.1 = bf16[4,4,8,256]{3,2,1,0:T(8,128)(2,1)S(1)} copy-done((bf16[4,4,8,256]{3,2,1,0:T(8,128)(2,1)S(1)}, bf16[4,4,8,256]{3,2,1,0:T(8,128)(2,1)}, u32[]{:S(2)}) %copy-start.1) | copy-done | bytes 65560
  4.1 32.6 %shard_map.67 = (bf16[32,4,8,256]{3,2,1,0:T(8,128)(2,1)S(1)}, f32[4,108]{1,0:T(4,128)S(1)}, f32[4,432]{1,0:T(4,128)S(1)}) custom-call(bf16[4,4,8,256]{3,2,1,0:T(8,128)(2,1)S(1)} %copy-done.1, bf16[32,4,8,256]{3,2,1,0:T(8,128)(2,1)S(1)} %copy-done, bf16[4,108]{1,0:T(4,128)(2,1)S(1)} %reshape.18.f1_ref, bf16[4,432]{1,0:T(4,128)(2,1)S(1)} %reshape.19.f2_ref), custom_call_target="tpu_custom_call" | custom-call | tf_op jit(solution)/shard_map/pallas_call | solution.py:434
  36.7 0.7 %reshape.20 = f32[432]{0:T(512)} reshape(f32[4,108]{1,0:T(4,128)S(1)} %get-tuple-element.7) | data formatting | bytes 3456 | tf_op jit(solution)/shard_map/reshape | solution.py:485
  37.3 0.7 %reshape.21 = f32[1728]{0:T(1024)} reshape(f32[4,432]{1,0:T(4,128)S(1)} %get-tuple-element.8) | data formatting | bytes 13824 | tf_op jit(solution)/shard_map/reshape | solution.py:485
  38.0 0.8 %copy.8 = bf16[32,4,8,256]{3,2,1,0:T(8,128)(2,1)} copy(bf16[32,4,8,256]{3,2,1,0:T(8,128)(2,1)S(1)} %get-tuple-element.12) | data formatting | bytes 1048576
Async XLA Ops:
  2.2 1.0 %copy-start = (bf16[32,4,8,256]{3,2,1,0:T(8,128)(2,1)S(1)}, bf16[32,4,8,256]{3,2,1,0:T(8,128)(2,1)}, u32[]{:S(2)}) copy-start(bf16[32,4,8,256]{3,2,1,0:T(8,128)(2,1)} %c_ref.1) | copy-start | bytes 1572868
  3.2 0.8 %copy-start.1 = (bf16[4,4,8,256]{3,2,1,0:T(8,128)(2,1)S(1)}, bf16[4,4,8,256]{3,2,1,0:T(8,128)(2,1)}, u32[]{:S(2)}) copy-start(bf16[4,4,8,256]{3,2,1,0:T(8,128)(2,1)} %v_ref.1) | copy-start | bytes 196612

commit v5 on v4

--- a/solution.py
+++ b/solution.py
@@ -117,9 +117,9 @@
 
 
 def fused_kernel(
-    n_space, n_samp, scale, v_ref, c_ref, f1_ref, f2_ref, act_ref, o1_ref, o2_ref,
+    n_space, n_samp, scale, v_hbm, c_hbm, f1_ref, f2_ref, act_ref, o1_ref, o2_ref,
     vp, cp, all1, all2,
-    turn, a1, a2, a3, hid, back, pre, t1, perm, acc1, acc2, act,
+    v_ref, c_ref, load_v, load_c, turn, a1, a2, a3, hid, back, pre, t1, perm, acc1, acc2, act,
     q1, q2, q3, rows1, wide1, rows2, wide2, tall3, vf, vrows,
     grad1, grad2, part1, part2, full1, full2, mine1, mine2,
     send_v, recv_v, send_c, recv_c, send_1, recv_1, send_2, recv_2,
@@ -128,6 +128,9 @@
     s = lax.axis_index("space")
     m = lax.axis_index("samp")
     size_x, size_y, size_z = v_ref.shape[1:]
+    loads = [pltpu.make_async_copy(v_hbm, v_ref, load_v), pltpu.make_async_copy(c_hbm, c_ref, load_c)]
+    for load in loads:
+        load.start()
 
     vp[...] = jnp.zeros_like(vp)
 
@@ -161,6 +164,9 @@
 
     turn[...] = one_hot_rows(C2, size_y)
     turn_v = one_hot_rows(CIN, size_y)
+
+    for load in loads:
+        load.wait()
 
     def centre(x, carry):
         value = c_ref[:, x].astype(F32).reshape(C2 * size_y, size_z).astype(BF16)
@@ -417,6 +423,7 @@
 
 
 VMEM = pl.BlockSpec(memory_space=pltpu.VMEM)
+HBM = pl.BlockSpec(memory_space=pltpu.HBM)
 
 
 def on_device(n_space, n_samp, volume, filters_one, filters_two, cotangent):
@@ -438,13 +445,17 @@
             jax.ShapeDtypeStruct(piece1, F32),
             jax.ShapeDtypeStruct(piece2, F32),
         ],
-        in_specs=[VMEM] * 4,
+        in_specs=[HBM, HBM, VMEM, VMEM],
         out_specs=[VMEM] * 3,
         scratch_shapes=[
             pltpu.VMEM((size_x + 6, size_y + 8, CIN, size_z), BF16),
             pltpu.VMEM((size_x + 2, size_y + 2, C2, size_z), BF16),
             pltpu.VMEM((n_samp, *piece1), BF16),
             pltpu.VMEM((n_space, *piece2), BF16),
+            pltpu.VMEM(volume.shape, BF16),
+            pltpu.VMEM(cotangent.shape, BF16),
+            pltpu.SemaphoreType.DMA(()),
+            pltpu.SemaphoreType.DMA(()),
             pltpu.VMEM((C2 * size_y, C2 * size_y), BF16),
             pltpu.VMEM((48 * high_y, 192), BF16),
             pltpu.VMEM((192, 192), BF16),

time: 39 us -> 39.2 us (level)
  no operation moved by 1% of the time
where the time goes in v5:
time: 39.2 us; the launch traced here: 38.9 us
  Pallas kernels  32.7 us (83%)
  local copies, waits for them, and re-layouts  5.55 us (14%)
  between operations  0.64 us (2%)
    pallas_call x1, Pallas kernels, on_device(): pl.pallas_call(functools.partial(fused_kernel, n_space, n_samp, scale), o...  32.7 us
    unnamed x5, local copies, waits for them, and re-layouts  2.68 us
    reshape x2, local copies, waits for them, and re-layouts, on_device(): return (activation, out1.reshape(len1), out2.reshape(len2))  1.34 us

profile of v5, /device:TPU:0, one launch (start us, length us, event | category | flops | bytes accessed | tf_op | source)
XLA Modules:
  0.0 38.9 jit_solution(6216390811740885352)
XLA Ops:
  0.6 0.8 %reshape.18.f1_ref = bf16[4,108]{1,0:T(4,128)(2,1)S(1)} reshape(bf16[432]{0:T(512)(128)(2,1)} %param.5) | data formatting | bytes 1728 | tf_op jit(solution)/shard_map/reshape | solution.py:495
  1.4 0.8 %reshape.19.f2_ref = bf16[4,432]{1,0:T(4,128)(2,1)S(1)} reshape(bf16[1728]{0:T(1024)(128)(2,1)} %param.6) | data formatting | bytes 6912 | tf_op jit(solution)/shard_map/reshape | solution.py:495
  2.2 0.0 copy-start
  2.2 1.0 %copy-done = bf16[32,4,8,256]{3,2,1,0:T(8,128)(2,1)S(1)} copy-done((bf16[32,4,8,256]{3,2,1,0:T(8,128)(2,1)S(1)}, bf16[32,4,8,256]{3,2,1,0:T(8,128)(2,1)}, u32[]{:S(2)}) %copy-start) | copy-done | bytes 524312
  3.2 0.0 copy-start.1
  3.2 0.8 %copy-done.1 = bf16[4,4,8,256]{3,2,1,0:T(8,128)(2,1)S(1)} copy-done((bf16[4,4,8,256]{3,2,1,0:T(8,128)(2,1)S(1)}, bf16[4,4,8,256]{3,2,1,0:T(8,128)(2,1)}, u32[]{:S(2)}) %copy-start.1) | copy-done | bytes 65560
  4.1 32.7 %shard_map.67 = (bf16[32,4,8,256]{3,2,1,0:T(8,128)(2,1)S(1)}, f32[4,108]{1,0:T(4,128)S(1)}, f32[4,432]{1,0:T(4,128)S(1)}) custom-call(bf16[4,4,8,256]{3,2,1,0:T(8,128)(2,1)S(1)} %copy-done.1, bf16[32,4,8,256]{3,2,1,0:T(8,128)(2,1)S(1)} %copy-done, bf16[4,108]{1,0:T(4,128)(2,1)S(1)} %reshape.18.f1_ref, bf16[4,432]{1,0:T(4,128)(2,1)S(1)} %reshape.19.f2_ref), custom_call_target="tpu_custom_call" | custom-call | tf_op jit(solution)/shard_map/pallas_call | solution.py:441
  36.8 0.7 %reshape.20 = f32[432]{0:T(512)} reshape(f32[4,108]{1,0:T(4,128)S(1)} %get-tuple-element.7) | data formatting | bytes 3456 | tf_op jit(solution)/shard_map/reshape | solution.py:496
  37.4 0.7 %reshape.21 = f32[1728]{0:T(1024)} reshape(f32[4,432]{1,0:T(4,128)S(1)} %get-tuple-element.8) | data formatting | bytes 13824 | tf_op jit(solution)/shard_map/reshape | solution.py:496
  38.1 0.8 %copy.8 = bf16[32,4,8,256]{3,2,1,0:T(8,128)(2,1)} copy(bf16[32,4,8,256]{3,2,1,0:T(8,128)(2,1)S(1)} %get-tuple-element.12) | data formatting | bytes 1048576
Async XLA Ops:
  2.2 1.0 %copy-start = (bf16[32,4,8,256]{3,2,1,0:T(8,128)(2,1)S(1)}, bf16[32,4,8,256]{3,2,1,0:T(8,128)(2,1)}, u32[]{:S(2)}) copy-start(bf16[32,4,8,256]{3,2,1,0:T(8,128)(2,1)} %c_hbm.1) | copy-start | bytes 1572868
  3.2 0.8 %copy-start.1 = (bf16[4,4,8,256]{3,2,1,0:T(8,128)(2,1)S(1)}, bf16[4,4,8,256]{3,2,1,0:T(8,128)(2,1)}, u32[]{:S(2)}) copy-start(bf16[4,4,8,256]{3,2,1,0:T(8,128)(2,1)} %v_hbm.1) | copy-start | bytes 196612
